TPU v7x, 128 devices: a whole 4x4x4 slice. The times are simulated.
128 devices in a mesh: row: 8 (over y_lo, x), col: 16 (over y_hi, z, core).
Axes of the slice: x: 4, y: 4 (y_hi: 2, y_lo: 2; y = y_hi * 2 + y_lo), z: 4, core: 2. Of those that a mesh axis runs over, the one named last changes fastest.
Arguments:
- density_block_entries: bfloat16 [64, 32, 128, 128], P('row', 'col'), as said below
- density_cols: int32 [64, 32], P('row', 'col'), may hold values from 0 to 63, as said below
- hamilton_values: bfloat16 [64, 32, 128, 128], P('row', 'col'), as said below
- hamilton_cols: int32 [64, 32], P('row', 'col'), may hold values from 0 to 63, as said below
- filter_cols: int32 [64, 64], P('row', 'col'), may hold values from 0 to 63, as said below
Outputs:
- squared_density: bfloat16 [64, 64, 128, 128], P('row', 'col')
- mixed_product: bfloat16 [64, 64, 128, 128], P('row', 'col')
- gradient: bfloat16 [64, 32, 128, 128], P('row', 'col')
Inputs may be any that keep to these rules, and one draw needn't show every extreme that they name: `density_cols`: in every block row, slots c * 2 to (c + 1) * 2 - 1 hold distinct block columns of c * 4 to (c + 1) * 4 - 1. The pattern is symmetric: j is listed in row i exactly when i is listed in row j. `hamilton_cols`: in every block row, slots c * 2 to (c + 1) * 2 - 1 hold distinct block columns of c * 4 to (c + 1) * 4 - 1. The pattern is symmetric: j is listed in row i exactly when i is listed in row j. `filter_cols`: in every block row, slots c * 4 to (c + 1) * 4 - 1 hold distinct block columns of c * 4 to (c + 1) * 4 - 1. `density_block_entries`: the density matrix is symmetric: the block of row i and column j is the transpose of the block of row j and column i. `hamilton_values`: the Hamiltonian is symmetric: the block of row i and column j is the transpose of the block of row j and column i.
All inputs are finite; a program needn't handle non-finite values.
Results may differ from a plain program's by a relative error of at most 0.015.
Values may be sent and summed in bfloat16 or wider, within the bound.
A program may use at most 128 MiB of HBM per device.

v0:
```python
import jax
import jax.numpy as jnp
from jax import lax
from jax.sharding import PartitionSpec as P


def block_products(left_vals, left_cols, right_vals, right_cols):
    chosen = right_vals[left_cols]
    block_product_list = jnp.einsum(
        "sab,stbc->stac", left_vals, chosen, preferred_element_type=jnp.float32
    )
    block_size = left_vals.shape[-1]
    return (
        block_product_list.reshape(-1, block_size, block_size),
        right_cols[left_cols].reshape(-1),
    )


def to_slots(block_product_list, product_cols, targets):
    filter_picker = (targets[:, None] == product_cols[None, :]).astype(jnp.float32)
    return jnp.einsum(
        "wv,vug->wug", filter_picker, block_product_list, precision=lax.Precision.HIGHEST
    )


def local(density_block_entries, density_cols, hamilton_values, hamilton_cols, filter_cols):
    density_panel, density_panel_cols, hamilton_panel, hamilton_panel_cols = (
        lax.all_gather(density_block_entries, "row", axis=0, tiled=True),
        lax.all_gather(density_cols, "row", axis=0, tiled=True),
        lax.all_gather(hamilton_values, "row", axis=0, tiled=True),
        lax.all_gather(hamilton_cols, "row", axis=0, tiled=True),
    )
    piece_values = lax.all_gather(density_block_entries, "col", axis=1, tiled=True)
    piece_cols = lax.all_gather(density_cols, "col", axis=1, tiled=True)

    def left_row(row_data):
        left_vals, left_cols, square_targets, pattern_targets = row_data
        square_terms, square_cols = block_products(
            left_vals, left_cols, density_panel, density_panel_cols
        )
        mixed_terms, mixed_cols = block_products(
            left_vals, left_cols, hamilton_panel, hamilton_panel_cols
        )
        return (
            to_slots(square_terms, square_cols, square_targets),
            to_slots(mixed_terms, mixed_cols, square_targets),
            to_slots(mixed_terms, mixed_cols, pattern_targets),
        )

    additions = lax.map(left_row, (piece_values, piece_cols, filter_cols, density_cols))
    square_sum = additions[0]
    mixed_sum = additions[1]
    direct_term = additions[2]
    square_term = square_sum.astype(jnp.bfloat16)
    mixed_term = mixed_sum.astype(jnp.bfloat16)
    piece_values = lax.all_gather(square_term, "col", axis=1, tiled=True)
    piece_cols = lax.all_gather(filter_cols, "col", axis=1, tiled=True)

    def square_row(row_data):
        left_vals, left_cols, pattern_targets = row_data
        cubic_terms, cubic_cols = block_products(
            left_vals, left_cols, hamilton_panel, hamilton_panel_cols
        )
        return to_slots(cubic_terms, cubic_cols, pattern_targets)

    cubic_term = lax.map(square_row, (piece_values, piece_cols, density_cols))
    gradient = (3.0 * direct_term - 2.0 * cubic_term).astype(jnp.bfloat16)
    return (square_term, mixed_term, gradient)


def solution(mesh):
    in_specs = (
        P("row", "col", None, None),
        P("row", "col"),
        P("row", "col", None, None),
        P("row", "col"),
        P("row", "col"),
    )
    out_specs = (
        P("row", "col", None, None),
        P("row", "col", None, None),
        P("row", "col", None, None),
    )
    return jax.shard_map(local, mesh=mesh, in_specs=in_specs, out_specs=out_specs, check_vma=False)
```

profile of v0, /device:TPU:1, one launch (start us, length us, event | category | flops | bytes accessed | tf_op | source)
XLA Modules:
  0.0 841.7 jit_solution(7834979033704034745)
XLA Ops:
  11.0 27.3 %all-gather = s32[16,2,8]{2,1,0:T(2,128)S(1)} all-gather(s32[1,2,8]{2,1,0:T(2,128)} %bitcast.149), channel_id=1, replica_groups=mesh['row'=8,'col'=16] {'col'}, dimensions={0}, use_global_device_ids=true | all-gather | bytes 1088 | tf_op jit(solution)/shard_map/all_gather | solution.py:34
  38.3 16.5 %all-gather.1 = s32[8,8,2]{1,2,0:T(2,128)S(1)} all-gather(s32[1,8,2]{1,2,0:T(2,128)} %bitcast.150), channel_id=1, replica_groups=mesh['row'=8,'col'=16] {'row'}, dimensions={0}, use_global_device_ids=true | all-gather | bytes 576 | tf_op jit(solution)/shard_map/all_gather | solution.py:29
  54.9 12.9 %all-gather.2 = s32[8,8,2]{1,2,0:T(2,128)S(1)} all-gather(s32[1,8,2]{1,2,0:T(2,128)} %bitcast.154), channel_id=1, replica_groups=mesh['row'=8,'col'=16] {'row'}, dimensions={0}, use_global_device_ids=true | all-gather | bytes 576 | tf_op jit(solution)/shard_map/all_gather | solution.py:31
  67.9 50.4 %all-gather.9.cloned.1.call-done = bf16[64,2,128,128]{3,2,1,0:T(8,128)(2,1)} async-done(((bf16[8,2,128,128]{3,2,1,0:T(8,128)(2,1)}), bf16[64,2,128,128]{3,2,1,0:T(8,128)(2,1)}) %all-gather.9.cloned.1.call-update) | async-done | bytes 4194320 | tf_op jit(solution)/shard_map/all_gather | solution.py:28
  118.3 74.8 %all-gather.11.cloned.1.call-done = bf16[8,32,128,128]{3,2,1,0:T(8,128)(2,1)} async-done(((bf16[8,2,128,128]{3,2,1,0:T(8,128)(2,1)}), bf16[8,32,128,128]{3,2,1,0:T(8,128)(2,1)}) %all-gather.11.cloned.1.call-update) | async-done | bytes 8388624 | tf_op jit(solution)/shard_map/all_gather | solution.py:33
  193.1 302.4 %while.24 = (s32[]{:T(128)}, bf16[8,4,128,128]{3,2,1,0:T(8,128)(2,1)}, bf16[8,4,128,128]{3,2,1,0:T(8,128)(2,1)}, f32[8,2,128,128]{3,2,1,0:T(8,128)S(1)}, s32[8,4...) while((s32[]{:T(128)}, ...), condition=%wide.region_1.2_spmd, body=%wide.region_0.1_spmd.sunk | while | flops 662701824 | bytes 70393744 | solution.py:50
  495.6 20.3 %all-gather.3 = s32[16,4,8]{2,1,0:T(4,128)S(1)} all-gather(s32[1,4,8]{2,1,0:T(4,128)S(1)} %bitcast.151), channel_id=1, replica_groups=mesh['row'=8,'col'=16] {'col'}, dimensions={0}, use_global_device_ids=true | all-gather | bytes 2176 | tf_op jit(solution)/shard_map/all_gather | solution.py:57
  515.9 86.3 %all-gather.15.cloned.1.call-done = bf16[8,64,128,128]{3,2,1,0:T(8,128)(2,1)} async-done(((bf16[8,4,128,128]{3,2,1,0:T(8,128)(2,1)}), bf16[8,64,128,128]{3,2,1,0:T(8,128)(2,1)}) %all-gather.15.cloned.1.call-update) | async-done | bytes 16777232 | tf_op jit(solution)/shard_map/all_gather | solution.py:56
  602.4 231.9 %while.25 = (s32[]{:T(128)}, f32[8,2,128,128]{3,2,1,0:T(8,128)S(1)}, s32[8,2]{1,0:T(8,128)S(1)}, s32[8,64]{1,0:T(8,128)S(1)}, s32[64,2]{1,0:T(8,128)S(1)}, /*ind...) while((s32[]{:T(128)}, f32[8,2,128,128]{3,2,1,0:T(8,128)S(1)}, ...), condition=%wide.region_3.4_spmd, body=%wide.region_2.3_spmd.sunk | while | flops 587204032 | bytes 48635780 | solution.py:66
  608.4 7.4 fusion.84
  615.8 9.4 %copy.103 = f32[128,128,128]{2,0,1:T(8,128)} copy(f32[128,128,128]{1,2,0:T(8,128)} %bitcast.142) | data formatting | bytes 16777216 | tf_op jit(solution)/shard_map/while/body/eval_jaxpr/reshape | solution.py:14
  625.2 6.2 convolution_bitcast_fusion.11
  637.4 7.4 fusion.84
  644.8 9.4 %copy.103 = f32[128,128,128]{2,0,1:T(8,128)} copy(f32[128,128,128]{1,2,0:T(8,128)} %bitcast.142) | data formatting | bytes 16777216 | tf_op jit(solution)/shard_map/while/body/eval_jaxpr/reshape | solution.py:14
  654.2 6.2 convolution_bitcast_fusion.11
  666.4 7.4 fusion.84
  673.8 9.4 %copy.103 = f32[128,128,128]{2,0,1:T(8,128)} copy(f32[128,128,128]{1,2,0:T(8,128)} %bitcast.142) | data formatting | bytes 16777216 | tf_op jit(solution)/shard_map/while/body/eval_jaxpr/reshape | solution.py:14
  683.2 6.2 convolution_bitcast_fusion.11
  695.4 7.4 fusion.84
  702.8 9.4 %copy.103 = f32[128,128,128]{2,0,1:T(8,128)} copy(f32[128,128,128]{1,2,0:T(8,128)} %bitcast.142) | data formatting | bytes 16777216 | tf_op jit(solution)/shard_map/while/body/eval_jaxpr/reshape | solution.py:14
  712.1 6.2 convolution_bitcast_fusion.11
  724.4 7.4 fusion.84
  731.8 9.4 %copy.103 = f32[128,128,128]{2,0,1:T(8,128)} copy(f32[128,128,128]{1,2,0:T(8,128)} %bitcast.142) | data formatting | bytes 16777216 | tf_op jit(solution)/shard_map/while/body/eval_jaxpr/reshape | solution.py:14
  741.1 6.2 convolution_bitcast_fusion.11
  753.3 7.4 fusion.84
  760.7 9.4 %copy.103 = f32[128,128,128]{2,0,1:T(8,128)} copy(f32[128,128,128]{1,2,0:T(8,128)} %bitcast.142) | data formatting | bytes 16777216 | tf_op jit(solution)/shard_map/while/body/eval_jaxpr/reshape | solution.py:14
  770.1 6.2 convolution_bitcast_fusion.11
  782.3 7.4 fusion.84
  789.7 9.4 %copy.103 = f32[128,128,128]{2,0,1:T(8,128)} copy(f32[128,128,128]{1,2,0:T(8,128)} %bitcast.142) | data formatting | bytes 16777216 | tf_op jit(solution)/shard_map/while/body/eval_jaxpr/reshape | solution.py:14
  799.1 6.2 convolution_bitcast_fusion.11
  811.3 7.4 fusion.84
  818.7 9.4 %copy.103 = f32[128,128,128]{2,0,1:T(8,128)} copy(f32[128,128,128]{1,2,0:T(8,128)} %bitcast.142) | data formatting | bytes 16777216 | tf_op jit(solution)/shard_map/while/body/eval_jaxpr/reshape | solution.py:14
  (247 shorter events, 361.6 us)
Async XLA Ops:
  7.2 60.7 %all-gather.13.cloned.1.call-start = ((), (), s32[]{:S(2)}) async-start(), calls=%async_computation.2 | async-start | bytes 4718592 | tf_op jit(solution)/shard_map/all_gather | solution.py:30
  7.9 110.4 %all-gather.9.cloned.1.call-start = ((), (), s32[]{:S(2)}) async-start(), calls=%async_computation | async-start | bytes 4718592 | tf_op jit(solution)/shard_map/all_gather | solution.py:28
  8.6 184.4 %all-gather.11.cloned.1.call-start = ((), (), s32[]{:S(2)}) async-start(), calls=%async_computation.1 | async-start | bytes 8912896 | tf_op jit(solution)/shard_map/all_gather | solution.py:33
  9.4 592.9 %all-gather.15.cloned.1.call-start = ((), (), s32[]{:S(2)}) async-start(), calls=%async_computation.3 | async-start | bytes 17825792 | tf_op jit(solution)/shard_map/all_gather | solution.py:56
  193.1 302.4 %copy-start.1 = (s32[8,4]{0,1:T(4,128)S(1)}, s32[8,4]{0,1:T(4,128)}, u32[]{:S(2)}) copy-start(s32[8,4]{0,1:T(4,128)} %param.13) | copy-start | bytes 388
  212.0 3.8 copy-start
  249.8 3.8 copy-start
  287.6 3.8 copy-start
  325.4 3.8 copy-start
  363.2 3.8 copy-start
  401.0 3.8 copy-start
  438.8 3.8 copy-start
  476.6 3.8 copy-start
Sparse Core Ops, SparseCore 0:
  9.6 55.6 all-gather.12
  66.9 51.2 all-gather.8
  120.8 72.1 all-gather.10
  495.7 106.5 all-gather.14
where the time goes:
time: 845 us; the launch traced here: 842 us
  local copies, waits for them, and re-layouts  288 us (34%)
  matrix products  247 us (29%)
  waiting for transfers between devices  214 us (25%)
  blocking collectives  77 us (9%)
  between operations  13.8 us (2%)
    reshape x24, local copies, waits for them, and re-layouts, block_products(): block_product_list.reshape(-1, block_size, block_size)  161 us
    dot_general x24, matrix products, block_products(): jnp.einsum('sab,stbc->stac', left_vals, chosen, preferred_element_type=jn...  127 us
    dot_general x32, matrix products, to_slots(): jnp.einsum('wv,vug->wug', filter_picker, block_product_list, precision=la...  120 us
    gather x24, local copies, waits for them, and re-layouts, block_products(): chosen = right_vals[left_cols]  102 us
    all_gather x1, waiting for transfers between devices, local(): piece_values = lax.all_gather(square_term, 'col', axis=1, tiled=True)  86.3 us
    all_gather x1, waiting for transfers between devices, local(): lax.all_gather(density_block_entries, 'col', axis=1, tiled=True)  74.8 us
    all_gather x1, waiting for transfers between devices, local(): lax.all_gather(density_block_entries, 'row', axis=0, tiled=True)  50.4 us
    all_gather x1, blocking collectives, local(): piece_cols = lax.all_gather(density_cols, 'col', axis=1, tiled=True)  27.3 us
  transfers between devices with their start and end apart: 4, of which 3 were waited for; matrix products, arithmetic and copies ran while one was open for 0% of the time, Pallas kernels for 0%

commit v1 on v0

v1 whole, which is shorter than its diff:
```python
import jax
import jax.numpy as jnp
from jax import lax
from jax.experimental import pallas as pl
from jax.experimental.pallas import tpu as pltpu
from jax.sharding import PartitionSpec as P

MESH = pl.DeviceIdType.MESH
BF16, F32 = jnp.bfloat16, jnp.float32
BS = 128
RB, CB = 8, 4
NR, NC = 8, 16
KS = 2
HALF = 4 * KS * BS
IND = 4 * KS * CB
SH = HALF + IND
ROWS, COLS, CHUNK = RB * BS, CB * BS, RB * BS


def remote(src, dst, send, recv, dev):
    return pltpu.make_async_remote_copy(
        src_ref=src, dst_ref=dst, send_sem=send, recv_sem=recv,
        device_id=dev, device_id_type=MESH,
    )


def kernel(dv, di, hv, hi, filt, dcols, s_out, m_out, g_out,
           Dcol, Hcol, Drow, Srow, relay, Ld, Rd, Hd, accS, accM, accC,
           loc, xs, xr, zs, zr, hs, hr, ts, tr, cs, cr, es, er, us, ur, vs, vr):
    row, col = lax.axis_index("row"), lax.axis_index("col")
    x, ylo = row % 4, row // 4
    core, z, yhi = col % 2, (col // 2) % 4, col // 8

    def ridx(f, d):
        yy = (1 - ylo) if f else ylo
        return yy * 4 + (x + d + 4) % 4

    def cidx(f, d, other=False):
        yy = (1 - yhi) if f else yhi
        cc = (1 - core) if other else core
        return yy * 8 + ((z + d + 4) % 4) * 2 + cc

    xp, xm = (ridx(0, 1), col), (ridx(0, -1), col)
    zp, zm = (row, cidx(0, 1)), (row, cidx(0, -1))
    ylod = (ridx(1, 0), col)
    yind = (ridx(1, 0), cidx(1, 0))
    twin = (row, cidx(0, 0, True))

    local = [
        pltpu.make_async_copy(dv, Dcol.at[row, :, pl.ds(0, HALF), :], loc.at[0]),
        pltpu.make_async_copy(di, Dcol.at[row, :, pl.ds(HALF, IND), :], loc.at[1]),
        pltpu.make_async_copy(dv, Drow.at[col, :, pl.ds(0, HALF), :], loc.at[2]),
        pltpu.make_async_copy(di, Drow.at[col, :, pl.ds(HALF, IND), :], loc.at[3]),
        pltpu.make_async_copy(hv, Hcol.at[row, :, pl.ds(0, HALF), :], loc.at[4]),
        pltpu.make_async_copy(hi, Hcol.at[row, :, pl.ds(HALF, IND), :], loc.at[5]),
    ]
    for c in local:
        c.start()
    barrier = pltpu.get_barrier_semaphore()
    for dev in (xp, xm, zp, zm, ylod, yind, twin):
        pl.semaphore_signal(barrier, inc=1, device_id=dev, device_id_type=MESH)
    accS[...] = jnp.zeros_like(accS)
    accM[...] = jnp.zeros_like(accM)
    accC[...] = jnp.zeros_like(accC)
    for c in local:
        c.wait()
    pl.semaphore_wait(barrier, 7)

    sends = []

    def push(ref, idx, half, send, recv, dev):
        view = ref.at[idx] if half is None else ref.at[idx, half]
        c = remote(view, view, send, recv, dev)
        c.start()
        sends.append(c)

    def got(ref, idx, half, recv):
        view = ref.at[idx] if half is None else ref.at[idx, half]
        remote(view, view, recv, recv, twin).wait_recv()

    X = lambda i: (xs.at[i], xr.at[i])
    Z = lambda i: (zs.at[i], zr.at[i])
    H = lambda i: (hs.at[i], hr.at[i])
    T = lambda i: (ts.at[i], tr.at[i])
    C = lambda i: (cs.at[i], cr.at[i])
    E = lambda i: (es.at[i], er.at[i])
    U = lambda i: (us.at[i], ur.at[i])
    V = lambda i: (vs.at[i], vr.at[i])

    def tslot(f, d):
        return (4 if f else 0) + (d + 4) % 4

    def twin_push(ref, S, f, d):
        push(ref, cidx(f, d), None, *S(tslot(f, d)), twin)

    def twin_got(ref, R, f, d):
        got(ref, cidx(f, d, True), None, R.at[tslot(f, d)])

    push(Dcol, row, 0, *X(0), ylod)
    push(Dcol, row, 1, *X(1), ylod)
    push(Dcol, row, None, *X(2), xp)
    push(Dcol, row, None, *X(3), xm)
    push(Drow, col, None, *Z(2), zp)
    push(Drow, col, None, *Z(3), zm)
    twin_push(Drow, C, 0, 0)

    P_ = ridx(1, 0)
    for h in (0, 1):
        got(Dcol, P_, h, xr.at[h])
        c = remote(Dcol.at[P_, h], Drow.at[col, h], zs.at[h], zr.at[h], yind)
        c.start()
        sends.append(c)
    push(Dcol, P_, None, *X(4), xp)
    push(Dcol, P_, None, *X(5), xm)
    got(Dcol, ridx(0, -1), None, xr.at[2])
    push(Dcol, ridx(0, -1), 0, *X(6), xp)
    got(Dcol, ridx(0, 1), None, xr.at[3])
    push(Dcol, ridx(0, 1), 1, *X(7), xm)
    got(Drow, cidx(0, -1), None, zr.at[2])
    push(Drow, cidx(0, -1), 0, *Z(6), zp)
    twin_push(Drow, C, 0, -1)
    got(Drow, cidx(0, 1), None, zr.at[3])
    push(Drow, cidx(0, 1), 1, *Z(7), zm)
    twin_push(Drow, C, 0, 1)
    Q_ = cidx(1, 0)
    got(Drow, Q_, 0, zr.at[0])
    push(Drow, Q_, 0, *Z(10), zp)
    push(Drow, Q_, 0, *Z(11), zm)
    got(Drow, Q_, 1, zr.at[1])
    push(Drow, Q_, 1, *Z(12), zp)
    push(Drow, Q_, 1, *Z(13), zm)
    twin_push(Drow, C, 1, 0)
    got(Dcol, ridx(1, -1), None, xr.at[4])
    push(Dcol, ridx(1, -1), 0, *X(8), xp)
    got(Dcol, ridx(1, 1), None, xr.at[5])
    push(Dcol, ridx(1, 1), 1, *X(9), xm)
    push(Hcol, row, None, *H(0), ylod)
    push(Hcol, row, None, *H(2), xp)
    push(Hcol, row, None, *H(3), xm)
    got(Drow, cidx(1, -1), 0, zr.at[10])
    got(Drow, cidx(1, -1), 1, zr.at[12])
    push(Drow, cidx(1, -1), 0, *Z(8), zp)
    twin_push(Drow, C, 1, -1)
    got(Drow, cidx(1, 1), 0, zr.at[11])
    got(Drow, cidx(1, 1), 1, zr.at[13])
    push(Drow, cidx(1, 1), 1, *Z(9), zm)
    twin_push(Drow, C, 1, 1)
    for f in (0, 1):
        for d in (0, -1, 1):
            twin_got(Drow, cr, f, d)

    def spread(src, idx, dst, lane):
        def body(half, carry):
            for ii in range(4):
                b0 = src[idx, half, pl.ds(ii * 256, BS), :]
                b1 = src[idx, half, pl.ds(ii * 256 + BS, BS), :]
                at = pl.ds(pl.multiple_of(half * 512 + ii * BS, BS), BS)
                ind = src[idx, half, pl.ds(HALF, IND), :].astype(F32)
                for t in range(CB):
                    k = ii * 8 + t
                    i0 = jnp.broadcast_to(ind[k:k + 1], (16, BS)).astype(BF16)
                    i1 = jnp.broadcast_to(ind[k + 4:k + 5], (16, BS)).astype(BF16)
                    out = b0.reshape(8, 16, BS) * i0[None] + b1.reshape(8, 16, BS) * i1[None]
                    dst[at, pl.ds(lane + t * BS, BS)] = out.reshape(BS, BS)
            return carry
        lax.fori_loop(0, 2, body, 0)

    def mm(acc, left, right):
        def body(t, carry):
            at = pl.ds(pl.multiple_of(t * 512, 512), 512)
            acc[at, :] += jnp.dot(left[at, :], right[...], preferred_element_type=F32)
            return carry
        lax.fori_loop(0, ROWS // 512, body, 0)

    def left_panel(k):
        spread(Drow, 2 * k, Ld, 0)
        spread(Drow, 2 * k + 1, Ld, COLS)

    dz = (z - x + 4) % 4
    o0 = (dz // 2) * (1 - dz % 2)
    o1 = 1 + 2 * (dz // 2)
    o2 = 4 - o0 - o1

    def order(n):
        b = n // 2
        e0 = (1 - b % 2) * (1 - b // 2)
        e1 = (b % 2) * (1 - b // 2)
        e2 = (1 - b % 2) * (b // 2)
        e3 = (b % 2) * (b // 2)
        return (n % 2) * 4 + (x + e0 * o0 + e1 * o1 + e2 * o2 + e3 * 2 + 4) % 4

    def s_chunk(n, carry):
        k = order(n)
        left_panel(k)
        spread(Dcol, k, Rd, 0)
        mm(accS, Ld, Rd)
        return carry

    lax.fori_loop(0, 4, s_chunk, 0)
    got(Drow, cidx(0, 2), 0, zr.at[6])
    got(Drow, cidx(0, 2), 1, zr.at[7])
    twin_push(Drow, C, 0, 2)
    got(Dcol, ridx(0, 2), 0, xr.at[6])
    got(Dcol, ridx(0, 2), 1, xr.at[7])
    got(Dcol, ridx(1, 2), 0, xr.at[8])
    got(Dcol, ridx(1, 2), 1, xr.at[9])
    got(Drow, cidx(1, 2), 0, zr.at[8])
    got(Drow, cidx(1, 2), 1, zr.at[9])
    twin_push(Drow, C, 1, 2)
    twin_got(Drow, cr, 0, 2)
    twin_got(Drow, cr, 1, 2)
    lax.fori_loop(4, 8, s_chunk, 0)

    Srow[col] = accS[...].astype(BF16).reshape(2, ROWS // 2, COLS)
    push(Srow, col, None, *U(2), zp)
    push(Srow, col, None, *U(3), zm)
    c0 = remote(Srow.at[col, 0], relay.at[0], es.at[0], er.at[0], ylod)
    c1 = remote(Srow.at[col, 1], relay.at[1], es.at[1], er.at[1], yind)
    for c in (c0, c1):
        c.start()
        sends.append(c)
    twin_push(Srow, V, 0, 0)

    got(Hcol, P_, None, hr.at[0])
    push(Hcol, P_, None, *H(4), xp)
    push(Hcol, P_, None, *H(5), xm)
    got(Hcol, ridx(0, -1), None, hr.at[2])
    push(Hcol, ridx(0, -1), 0, *H(6), xp)
    got(Hcol, ridx(0, 1), None, hr.at[3])
    push(Hcol, ridx(0, 1), 1, *H(7), xm)

    def m_chunk(k):
        left_panel(k)
        spread(Hcol, k, Hd.at[k], 0)
        mm(accM, Ld, Hd.at[k])

    def m_near(n, carry):
        m_chunk((n % 2) * 4 + (x + n // 2 + (n // 2) // 2) % 4)
        return carry

    def m_near_own(n, carry):
        b = n // 2
        m_chunk(((ylo + n) % 2) * 4 + (x + b + b // 2) % 4)
        return carry

    m_chunk(row)
    got(relay, 0, None, er.at[0])
    c = remote(relay.at[0], Srow.at[col, 0], us.at[0], ur.at[0], yind)
    c.start()
    sends.append(c)
    got(relay, 1, None, er.at[1])
    c = remote(relay.at[1], Srow.at[Q_, 1], us.at[1], ur.at[1], ylod)
    c.start()
    sends.append(c)
    m_chunk(P_)
    got(Hcol, ridx(1, -1), None, hr.at[4])
    push(Hcol, ridx(1, -1), 0, *H(8), xp)
    got(Hcol, ridx(1, 1), None, hr.at[5])
    push(Hcol, ridx(1, 1), 1, *H(9), xm)
    got(Srow, cidx(0, -1), None, ur.at[2])
    push(Srow, cidx(0, -1), 0, *U(6), zp)
    twin_push(Srow, V, 0, -1)
    got(Srow, cidx(0, 1), None, ur.at[3])
    push(Srow, cidx(0, 1), 1, *U(7), zm)
    twin_push(Srow, V, 0, 1)
    got(Srow, Q_, 0, ur.at[0])
    got(Srow, Q_, 1, ur.at[1])
    push(Srow, Q_, None, *U(4), zp)
    push(Srow, Q_, None, *U(5), zm)
    twin_push(Srow, V, 1, 0)

    def m_mid(n, carry):
        m_chunk((n % 2) * 4 + (x + 1 + 2 * (n // 2)) % 4)
        return carry

    lax.fori_loop(0, 4, m_mid, 0)
    got(Hcol, ridx(0, 2), 0, hr.at[6])
    got(Hcol, ridx(0, 2), 1, hr.at[7])
    got(Hcol, ridx(1, 2), 0, hr.at[8])
    got(Hcol, ridx(1, 2), 1, hr.at[9])

    def m_far(n, carry):
        m_chunk(n * 4 + (x + 2) % 4)
        return carry

    lax.fori_loop(0, 2, m_far, 0)

    def pick(acc, i, which):
        at = pl.ds(pl.multiple_of(i * BS, BS), BS)
        place = jnp.broadcast_to(which, (BS, BS))
        out = acc[at, pl.ds(0, BS)]
        for t in range(1, CB):
            out = jnp.where(place == t, acc[at, pl.ds(t * BS, BS)], out)
        return out

    def filtered(i, carry):
        for w in range(CB):
            which = filt[i, w:w + 1, :]
            s_out[i * CB + w] = pick(accS, i, which).astype(BF16)
            m_out[i * CB + w] = pick(accM, i, which).astype(BF16)
        return carry

    lax.fori_loop(0, RB, filtered, 0)

    def c_chunk(f, d):
        for c in (0, 1):
            k = cidx(f, d) - core + c
            def body(t, carry, k=k, c=c):
                at = pl.ds(pl.multiple_of(t * 512, 512), 512)
                accC[at, :] += jnp.dot(
                    Srow[k, t], Hd[k // 2, pl.ds(c * COLS, COLS), :],
                    preferred_element_type=F32)
                return carry
            lax.fori_loop(0, 2, body, 0)

    twin_got(Srow, vr, 0, 0)
    c_chunk(0, 0)
    twin_got(Srow, vr, 0, -1)
    c_chunk(0, -1)
    twin_got(Srow, vr, 0, 1)
    c_chunk(0, 1)
    twin_got(Srow, vr, 1, 0)
    c_chunk(1, 0)
    got(Srow, cidx(0, 2), 0, ur.at[6])
    got(Srow, cidx(0, 2), 1, ur.at[7])
    twin_push(Srow, V, 0, 2)
    got(Srow, cidx(1, -1), None, ur.at[4])
    push(Srow, cidx(1, -1), 0, *U(8), zp)
    twin_push(Srow, V, 1, -1)
    got(Srow, cidx(1, 1), None, ur.at[5])
    push(Srow, cidx(1, 1), 1, *U(9), zm)
    twin_push(Srow, V, 1, 1)
    twin_got(Srow, vr, 0, 2)
    c_chunk(0, 2)
    twin_got(Srow, vr, 1, -1)
    c_chunk(1, -1)
    twin_got(Srow, vr, 1, 1)
    c_chunk(1, 1)
    got(Srow, cidx(1, 2), 0, ur.at[8])
    got(Srow, cidx(1, 2), 1, ur.at[9])
    twin_push(Srow, V, 1, 2)
    twin_got(Srow, vr, 1, 2)
    c_chunk(1, 2)

    def gradient(i, carry):
        for s in range(KS):
            which = dcols[i, s:s + 1, :]
            g_out[i * KS + s] = (3.0 * pick(accM, i, which) - 2.0 * pick(accC, i, which)).astype(BF16)
        return carry

    lax.fori_loop(0, RB, gradient, 0)
    for c in sends:
        c.wait_send()


def local(density, density_cols, hamilton, hamilton_cols, filter_cols):
    base = lax.axis_index("col") * CB

    def indicators(cols):
        hit = cols[:, :, None] == base + jnp.arange(CB, dtype=jnp.int32)
        hit = jnp.broadcast_to(hit[..., None], (RB, KS, CB, BS))
        return hit.astype(BF16).reshape(2, IND, BS)

    def places(cols):
        return jnp.broadcast_to((cols - base)[:, :, None], cols.shape + (BS,))

    def values(v):
        return v.reshape(2, HALF, BS)

    hbm = pl.BlockSpec(memory_space=pl.ANY)
    vmem = pl.BlockSpec(memory_space=pltpu.VMEM)
    dma = lambda n: pltpu.SemaphoreType.DMA((n,))
    s, m, g = pl.pallas_call(
        kernel,
        out_shape=(
            jax.ShapeDtypeStruct((RB * CB, BS, BS), BF16),
            jax.ShapeDtypeStruct((RB * CB, BS, BS), BF16),
            jax.ShapeDtypeStruct((RB * KS, BS, BS), BF16),
        ),
        in_specs=[hbm] * 4 + [vmem] * 2,
        out_specs=(vmem,) * 3,
        scratch_shapes=[
            pltpu.VMEM((NR, 2, SH, BS), BF16),
            pltpu.VMEM((NR, 2, SH, BS), BF16),
            pltpu.VMEM((NC, 2, SH, BS), BF16),
            pltpu.VMEM((NC, 2, ROWS // 2, COLS), BF16),
            pltpu.VMEM((2, ROWS // 2, COLS), BF16),
            pltpu.VMEM((ROWS, CHUNK), BF16),
            pltpu.VMEM((CHUNK, COLS), BF16),
            pltpu.VMEM((NR, CHUNK, COLS), BF16),
            pltpu.VMEM((ROWS, COLS), F32),
            pltpu.VMEM((ROWS, COLS), F32),
            pltpu.VMEM((ROWS, COLS), F32),
            dma(6),
            dma(10), dma(10), dma(14), dma(14), dma(10), dma(10), dma(1), dma(1),
            dma(8), dma(8), dma(2), dma(2), dma(10), dma(10), dma(8), dma(8),
        ],
        compiler_params=pltpu.CompilerParams(
            collective_id=0, has_side_effects=True, vmem_limit_bytes=66_000_000),
    )(values(density), indicators(density_cols), values(hamilton),
      indicators(hamilton_cols), places(filter_cols), places(density_cols))
    return (s.reshape(RB, CB, BS, BS), m.reshape(RB, CB, BS, BS), g.reshape(RB, KS, BS, BS))


def solution(mesh):
    blocks, cols = P("row", "col", None, None), P("row", "col")
    return jax.shard_map(
        local, mesh=mesh, in_specs=(blocks, cols, blocks, cols, cols),
        out_specs=(blocks,) * 3, check_vma=False)
```

time: 845 us -> 149 us (0.18)
  local copies, waits for them, and re-layouts: 288 us -> 8.48 us
  matrix products: 247 us -> 0 us
  waiting for transfers between devices: 214 us -> 0 us
  Pallas kernels: 0 us -> 139 us
  blocking collectives: 77 us -> 0 us
  between operations: 13.8 us -> 0.69 us
    dot_general x56 -> x0, matrix products: 247 us -> none  [the longest x24 127 us: block_products(): jnp.einsum('sab,stbc->stac', left_vals, chosen, preferred_element_type=jn...]
    all_gather x4 -> x0, waiting for transfers between devices: 211 us -> none  [the longest x1 86.3 us: local(): piece_values = lax.all_gather(square_term, 'col', axis=1, tiled=True)]
    reshape x24 -> x0, local copies, waits for them, and re-layouts: 161 us -> none  [block_products(): block_product_list.reshape(-1, block_size, block_size)]
    pallas_call x0 -> x1, Pallas kernels: none -> 139 us  [local(): pl.pallas_call(kernel, out_shape=(jax.ShapeDtypeStruct((RB * CB, BS, BS),...]
    gather x48 -> x0, local copies, waits for them, and re-layouts: 116 us -> none  [the longest x24 102 us: block_products(): chosen = right_vals[left_cols]]
    all_gather x4 -> x0, blocking collectives: 77 us -> none  [the longest x1 27.3 us: local(): piece_cols = lax.all_gather(density_cols, 'col', axis=1, tiled=True)]
  transfers between devices with their start and end apart: 4 -> 0, of which waited for: 3 -> 0; matrix products, arithmetic and copies ran while one was open for 0% -> 0% of each run, Pallas kernels for 0% -> 0%
where the time goes in v1:
time: 149 us
  Pallas kernels  139 us (93%)
  local copies, waits for them, and re-layouts  8.48 us (6%)
    pallas_call x1, Pallas kernels, local(): pl.pallas_call(kernel, out_shape=(jax.ShapeDtypeStruct((RB * CB, BS, BS),...  139 us
    unnamed x15, local copies, waits for them, and re-layouts  5.42 us

profile of v1, /device:TPU:1, one launch (start us, length us, event | category | flops | bytes accessed | tf_op | source)
XLA Modules:
  0.0 148.6 jit_solution(9351544928878259829)
XLA Ops:
  0.6 0.0 copy-start.2
  0.6 0.0 copy-start.3
  0.7 0.6 copy-done.2
  1.3 0.0 copy-done.3
  1.3 0.1 copy.14
  1.4 0.1 copy.15
  1.5 0.0 copy-start.4
  1.5 0.7 broadcast_in_dim.11.dcols
  2.2 0.0 copy-done.4
  2.2 0.1 copy.13
  2.3 0.1 copy.12
  2.3 0.1 compare_convert_fusion
  2.4 0.1 reshape.51
  2.5 0.1 reshape.50
  2.6 0.7 broadcast_in_dim.10.filt
  3.3 0.7 broadcast_in_dim.8.di
  4.0 0.7 broadcast_in_dim.9.hi
  4.7 139.3 %shard_map.76 = (bf16[32,128,128]{2,1,0:T(8,128)(2,1)}, bf16[32,128,128]{2,1,0:T(8,128)(2,1)}, bf16[16,128,128]{2,1,0:T(8,128)(2,1)}) custom-call(bf16[2,1024,128]{2,1,0:T(8,128)(2,1)} %bitcast.7, bf16[2,32,128]{2,1,0:T(8,128)(2,1)} %broadcast_in_dim.8.di, bf16[2,1024,128]{2,1,0:T(8,128)(2,1)} %bitcast.8, bf16[2,32,128]{2,1,0:T(8,128)(2,1)} %broadcast_in_dim.9.hi, ...), custom_call_target="tpu_custom_call" | custom-call | tf_op jit(solution)/shard_map/pallas_call | solution.py:373
  144.0 0.0 copy-start
  144.0 2.4 %copy.19 = bf16[8,4,128,128]{3,2,1,0:T(8,128)(2,1)} copy(bf16[8,4,128,128]{3,2,1,0:T(8,128)(2,1)} %bitcast.6) | data formatting | bytes 2097152
  146.4 0.0 copy-done
  146.4 0.0 copy-start.1
  146.4 1.0 copy.20
  147.4 0.4 copy-done.1
  147.8 0.8 copy.21
  (3 shorter events, 0.0 us)
Async XLA Ops:
  0.6 0.7 copy-start.2
  0.6 0.7 copy-start.3
  1.5 0.7 copy-start.4
  144.0 2.4 %copy-start = (bf16[32,128,128]{2,1,0:T(8,128)(2,1)S(1)}, bf16[32,128,128]{2,1,0:T(8,128)(2,1)}, u32[]{:S(2)}) copy-start(bf16[32,128,128]{2,1,0:T(8,128)(2,1)} %get-tuple-element.7) | copy-start | bytes 3145732
  146.4 1.4 copy-start.1

commit v2 on v0

v2 whole, which is shorter than its diff:
```python
import jax
import jax.numpy as jnp
from jax import lax
from jax.experimental import pallas as pl
from jax.experimental.pallas import tpu as pltpu
from jax.sharding import PartitionSpec as P

MESH = pl.DeviceIdType.MESH
BF16, F32 = jnp.bfloat16, jnp.float32
BS = 128
RB, CB = 8, 4
NR, NC = 8, 16
KS = 2
HALF = 4 * KS * BS
IND = 4 * KS * CB
SH = HALF + IND
NP = 8
JP = BS // NP
ROWS, COLS, CHUNK = RB * BS, CB * BS, RB * BS


def remote(src, dst, send, recv, dev):
    return pltpu.make_async_remote_copy(
        src_ref=src, dst_ref=dst, send_sem=send, recv_sem=recv,
        device_id=dev, device_id_type=MESH,
    )


def kernel(dv, di, hv, hi, filt, dcols, s_out, m_out, g_out,
           Dcol, Hcol, Drow, Htw, Hti, Sown, Stw, Dd, Rd, Hr0, Hr1, accS, accM, CT,
           PB, Al, Ar, Bl, Br, Y, cub,
           loc, xs, xr, zs, zr, hs, hr, cs, cr, ts, tr, as_, ar, bs, br, ys, yr):
    row, col = lax.axis_index("row"), lax.axis_index("col")
    x, ylo = row % 4, row // 4
    core, z, yhi = col % 2, (col // 2) % 4, col // 8

    def ridx(f, d):
        yy = (1 - ylo) if f else ylo
        return yy * 4 + (x + d + 4) % 4

    def cidx(f, d, other=False):
        yy = (1 - yhi) if f else yhi
        cc = (1 - core) if other else core
        return yy * 8 + ((z + d + 4) % 4) * 2 + cc

    xp, xm = (ridx(0, 1), col), (ridx(0, -1), col)
    zp, zm = (row, cidx(0, 1)), (row, cidx(0, -1))
    ylod = (ridx(1, 0), col)
    yind = (ridx(1, 0), cidx(1, 0))
    yhid = (row, cidx(1, 0))
    twin = (row, cidx(0, 0, True))

    first = [
        pltpu.make_async_copy(dv, Dcol.at[row, :, pl.ds(0, HALF), :], loc.at[0]),
        pltpu.make_async_copy(di, Dcol.at[row, :, pl.ds(HALF, IND), :], loc.at[1]),
        pltpu.make_async_copy(hi, Dcol.at[row, :, pl.ds(SH, IND), :], loc.at[2]),
        pltpu.make_async_copy(dv, Drow.at[col, :, pl.ds(0, HALF), :], loc.at[3]),
        pltpu.make_async_copy(di, Drow.at[col, :, pl.ds(HALF, IND), :], loc.at[4]),
    ]
    later = [
        pltpu.make_async_copy(hv.at[:, :, q], Hcol.at[q, row], loc.at[5 + q])
        for q in range(NP)
    ]
    for c in first + later:
        c.start()
    barrier = pltpu.get_barrier_semaphore()
    for dev in (xp, xm, zp, zm, ylod, yind, yhid, twin):
        pl.semaphore_signal(barrier, inc=1, device_id=dev, device_id_type=MESH)
    for c in first:
        c.wait()
    pl.semaphore_wait(barrier, 8)

    sends = []

    def push(view, send, recv, dev, there=None):
        c = remote(view, view if there is None else there, send, recv, dev)
        c.start()
        sends.append(c)

    def got(view, recv):
        remote(view, view, recv, recv, twin).wait_recv()

    def sent(view, send):
        remote(view, view, send, send, twin).wait_send()

    def dc(f, d, half=None):
        k = ridx(f, d)
        return Dcol.at[k] if half is None else Dcol.at[k, half]

    def dr(f, d, half=None, other=False):
        k = cidx(f, d, other)
        return Drow.at[k] if half is None else Drow.at[k, half]

    def X(view, i, dev):
        push(view, xs.at[i], xr.at[i], dev)

    def Z(view, i, dev):
        push(view, zs.at[i], zr.at[i], dev)

    def to_twin(f, d):
        i = f * 4 + (d + 4) % 4
        push(dr(f, d), cs.at[i], cr.at[i], twin)

    def from_twin(f, d):
        got(dr(f, d, other=True), cr.at[f * 4 + (d + 4) % 4])

    X(dc(0, 0, 0), 0, ylod)
    X(dc(0, 0, 1), 1, ylod)
    X(dc(0, 0), 2, xp)
    X(dc(0, 0), 3, xm)
    Z(dr(0, 0), 2, zp)
    Z(dr(0, 0), 3, zm)
    to_twin(0, 0)
    accS[...] = jnp.zeros_like(accS)
    accM[...] = jnp.zeros_like(accM)
    for c in later:
        c.wait()

    for h in (0, 1):
        got(dc(1, 0, h), xr.at[h])
        push(Dcol.at[ridx(1, 0), h, pl.ds(0, SH)], zs.at[h], zr.at[h], yind, Drow.at[col, h])
    X(dc(1, 0), 4, xp)
    X(dc(1, 0), 5, xm)
    got(dc(0, -1), xr.at[2])
    X(dc(0, -1, 0), 6, xp)
    got(dc(0, 1), xr.at[3])
    X(dc(0, 1, 1), 7, xm)
    got(dr(0, -1), zr.at[2])
    Z(dr(0, -1, 0), 6, zp)
    to_twin(0, -1)
    got(dr(0, 1), zr.at[3])
    Z(dr(0, 1, 1), 7, zm)
    to_twin(0, 1)
    for h in (0, 1):
        got(dr(1, 0, h), zr.at[h])
        Z(dr(1, 0, h), 10 + 2 * h, zp)
        Z(dr(1, 0, h), 11 + 2 * h, zm)
    to_twin(1, 0)
    got(dc(1, -1), xr.at[4])
    X(dc(1, -1, 0), 8, xp)
    got(dc(1, 1), xr.at[5])
    X(dc(1, 1, 1), 9, xm)

    def hp(q, f, d, half=None):
        k = ridx(f, d)
        return Hcol.at[q, k] if half is None else Hcol.at[q, k, half]

    H_OWN = ((0, 0, None, 0, ylod), (0, 0, None, 1, xp), (0, 0, None, 2, xm))
    H_MID = ((1, 0, None, 3, xp), (1, 0, None, 4, xm), (0, -1, 0, 5, xp), (0, 1, 1, 6, xm))
    H_FAR = ((1, -1, 0, 7, xp), (1, 1, 1, 8, xm))

    def h_push(q, f, d, half, i, dev):
        view = hp(q, f, d, half)
        remote(view, view, hs.at[q * 9 + i], hr.at[q * 9 + i], dev).start()

    def h_own(q):
        for a in H_OWN:
            h_push(q, *a)

    def h_mid(q):
        got(hp(q, 1, 0), hr.at[q * 9])
        h_push(q, *H_MID[0])
        h_push(q, *H_MID[1])
        got(hp(q, 0, -1), hr.at[q * 9 + 1])
        h_push(q, *H_MID[2])
        got(hp(q, 0, 1), hr.at[q * 9 + 2])
        h_push(q, *H_MID[3])

    def h_far(q):
        got(hp(q, 1, -1), hr.at[q * 9 + 3])
        h_push(q, *H_FAR[0])
        got(hp(q, 1, 1), hr.at[q * 9 + 4])
        h_push(q, *H_FAR[1])

    def h_end(q):
        got(hp(q, 0, 2, 0), hr.at[q * 9 + 5])
        got(hp(q, 0, 2, 1), hr.at[q * 9 + 6])
        got(hp(q, 1, 2, 0), hr.at[q * 9 + 7])
        got(hp(q, 1, 2, 1), hr.at[q * 9 + 8])

    for q in range(3):
        h_own(q)
    got(dr(1, -1, 0), zr.at[10])
    got(dr(1, -1, 1), zr.at[12])
    Z(dr(1, -1, 0), 8, zp)
    to_twin(1, -1)
    got(dr(1, 1, 0), zr.at[11])
    got(dr(1, 1, 1), zr.at[13])
    Z(dr(1, 1, 1), 9, zm)
    to_twin(1, 1)
    for f in (0, 1):
        for d in (0, -1, 1):
            from_twin(f, d)

    def spread(block, ind, store):
        for ii in range(4):
            b0, b1 = block(ii * 2), block(ii * 2 + 1)
            n = b0.shape[0] // 16
            for t in range(CB):
                k = ii * 8 + t
                i0 = jnp.broadcast_to(ind[k:k + 1], (16, BS)).astype(BF16)
                i1 = jnp.broadcast_to(ind[k + 4:k + 5], (16, BS)).astype(BF16)
                out = b0.reshape(n, 16, BS) * i0[None] + b1.reshape(n, 16, BS) * i1[None]
                store(ii, t, out.reshape(n * 16, BS))

    def spread_d(src, k, put):
        def body(half, carry):
            ind = src[k, half, pl.ds(HALF, IND), :].astype(F32)

            def store(ii, t, v):
                put(pl.ds(pl.multiple_of(half * 512 + ii * BS, BS), BS), t, v)

            spread(lambda b: src[k, half, pl.ds(b * BS, BS), :], ind, store)
            return carry
        lax.fori_loop(0, 2, body, 0)

    def put_r(at, t, v):
        Rd[at, pl.ds(t * BS, BS)] = v

    dz = (z - x + 4) % 4
    o0 = (dz // 2) * (1 - dz % 2)
    o1 = 1 + 2 * (dz // 2)
    o2 = 4 - o0 - o1

    def order(n):
        b = n // 2
        e0 = (1 - b % 2) * (1 - b // 2)
        e1 = (b % 2) * (1 - b // 2)
        e2 = (1 - b % 2) * (b // 2)
        e3 = (b % 2) * (b // 2)
        return (n % 2) * 4 + (x + e0 * o0 + e1 * o1 + e2 * o2 + e3 * 2 + 4) % 4

    def s_chunk(n, carry):
        k = order(n)
        for c in (0, 1):
            def put(at, t, v, c=c):
                Dd[k, at, pl.ds(c * COLS + t * BS, BS)] = v
            spread_d(Drow, 2 * k + c, put)
        spread_d(Dcol, k, put_r)
        accS[...] += jnp.dot(Dd[k], Rd[...], preferred_element_type=F32)

        @pl.when(n == 3)
        def _():
            got(dr(0, 2, 0), zr.at[6])
            got(dr(0, 2, 1), zr.at[7])
            remote(dr(0, 2), dr(0, 2), cs.at[2], cr.at[2], twin).start()
            for f in (0, 1):
                got(dc(f, 2, 0), xr.at[6 + 2 * f])
                got(dc(f, 2, 1), xr.at[7 + 2 * f])
            h_mid(0)
            h_mid(1)
            got(dr(1, 2, 0), zr.at[8])
            got(dr(1, 2, 1), zr.at[9])
            remote(dr(1, 2), dr(1, 2), cs.at[6], cr.at[6], twin).start()
            from_twin(0, 2)
            from_twin(1, 2)

        @pl.when(n == 5)
        def _():
            h_far(0)
            h_own(3)
            h_mid(2)

        return carry

    lax.fori_loop(0, 8, s_chunk, 0)

    Sown[...] = accS[...].astype(BF16)
    push(Sown, ts.at[NP], tr.at[NP], twin, Stw)
    push(Dcol.at[:, 1 - core, pl.ds(SH, IND)], ts.at[NP + 1], tr.at[NP + 1], twin, Hti)
    h_far(1)
    got(Stw, tr.at[NP])
    got(Hti, tr.at[NP + 1])

    def pick(acc, i, which):
        at = pl.ds(pl.multiple_of(i * BS, BS), BS)
        place = jnp.broadcast_to(which, (BS, BS))
        out = acc[at, pl.ds(0, BS)]
        for t in range(1, CB):
            out = jnp.where(place == t, acc[at, pl.ds(t * BS, BS)], out)
        return out

    def filtered(acc, out, i):
        for w in range(CB):
            out[i * CB + w] = pick(acc, i, filt[i, w:w + 1, :]).astype(BF16)

    NT = (((1,), (1,)), ((), ()))

    def partials(q):
        def rows(m, carry):
            def put(ref):
                def store(ii, t, v):
                    at = pl.ds(pl.multiple_of(m * 64 + ii * JP, JP), JP)
                    ref[at, pl.ds(t * BS, BS)] = v
                return store
            own = Dcol[m, core, pl.ds(SH, IND), :].astype(F32)
            spread(lambda b: Hcol[q, m, core, b], own, put(Hr0))
            spread(lambda b: Htw[q, m, b], Hti[m].astype(F32), put(Hr1))
            return carry
        lax.fori_loop(0, 8, rows, 0)
        CT[q % 3] = (
            lax.dot_general(Hr0[...], Sown[...], NT, preferred_element_type=F32)
            + lax.dot_general(Hr1[...], Stw[...], NT, preferred_element_type=F32)
        )

    def extract(q, m, half, emit):
        ind = Drow[2 * m + core, half, pl.ds(HALF, IND), :].astype(F32)
        for ii in range(4):
            lanes = pl.ds((half * 4 + ii) * BS, BS)
            v = [CT[q % 3, pl.ds(pl.multiple_of(m * 64 + t * JP, JP), JP), lanes] for t in range(CB)]
            for s in range(KS):
                out = v[0]
                for t in range(1, CB):
                    k = ii * 8 + s * 4 + t
                    hit = jnp.broadcast_to(ind[k:k + 1], (JP, BS)) > 0.5
                    out = jnp.where(hit, v[t], out)
                emit(ii * KS + s, out)

    def chip(f, d):
        hh = (1 - yhi) if f else yhi
        return hh * 4 + (z + d + 4) % 4

    def rs_far(q):
        for f in (1, 0):
            m = chip(f, 2)
            for half, (dev, dst) in enumerate(((zp, Al), (zm, Ar))):
                def emit(b, v, half=half):
                    PB[q, m, half * 8 + b] = v.astype(BF16)
                extract(q, m, half, emit)
                i = q * 4 + f * 2 + half
                remote(PB.at[q, m, pl.ds(half * 8, 8)], dst.at[q, f], as_.at[i], ar.at[i], dev).start()

    def rs_near(q):
        for f in (1, 0):
            for side, (d, dev, src, dst) in enumerate(((1, zp, Al, Bl), (-1, zm, Ar, Br))):
                m = chip(f, d)
                i = q * 4 + f * 2 + side
                got(src.at[q, f], ar.at[i])
                for half in (0, 1):
                    def emit(b, v, half=half):
                        if half == side:
                            v = v + src[q, f, b].astype(F32)
                        PB[q, m, half * 8 + b] = v.astype(BF16)
                    extract(q, m, half, emit)
                remote(PB.at[q, m], dst.at[q, f], bs.at[i], br.at[i], dev).start()

    def rs_own(q):
        for f in (1, 0):
            m = chip(f, 0)
            got(Bl.at[q, f], br.at[q * 4 + f * 2])
            got(Br.at[q, f], br.at[q * 4 + f * 2 + 1])
            for half in (0, 1):
                def emit(b, v, half=half):
                    b = half * 8 + b
                    v = v + Bl[q, f, b].astype(F32) + Br[q, f, b].astype(F32)
                    if f:
                        PB[q, m, b] = v.astype(BF16)
                    else:
                        cub[b, pl.ds(pl.multiple_of(q * JP, JP), JP), :] = v
                extract(q, m, half, emit)
            if f:
                remote(PB.at[q, m], Y.at[q], ys.at[q], yr.at[q], yhid).start()

    def m_chunk(k, carry):
        def body(half, c):
            ind = Dcol[k, half, pl.ds(SH, IND), :].astype(F32)

            def store(ii, t, v):
                Rd[pl.ds(pl.multiple_of(half * 512 + ii * BS, BS), BS), pl.ds(t * BS, BS)] = v

            spread(lambda b: Hcol[:, k, half, b].reshape(BS, BS), ind, store)
            return c
        lax.fori_loop(0, 2, body, 0)
        accM[...] += jnp.dot(Dd[k], Rd[...], preferred_element_type=F32)
        return carry

    def step(q, carry):
        @pl.when(q < NP)
        def _():
            h_end(q)
            remote(Hcol.at[q, :, 1 - core], Htw.at[q], ts.at[q], tr.at[q], twin).start()

        @pl.when(q + 2 < NP)
        def _():
            h_far(q + 2)

        @pl.when(q + 3 < NP)
        def _():
            h_mid(q + 3)

        @pl.when(q + 4 < NP)
        def _():
            h_own(q + 4)

        @pl.when(q < NP)
        def _():
            filtered(accS, s_out, q)
            got(Htw.at[q], tr.at[q])
            partials(q)
            rs_far(q)

        @pl.when((q >= 1) & (q < NP + 1))
        def _():
            rs_near(q - 1)

        @pl.when(q >= 2)
        def _():
            rs_own(q - 2)

        @pl.when(q >= NP - 1)
        def _():
            lo = (q - NP + 1) * 3
            lax.fori_loop(lo, lo + 3 - (q - NP + 1) // 2, m_chunk, 0)

        return carry

    lax.fori_loop(0, NP + 2, step, 0)

    def m_rows(i, carry):
        filtered(accM, m_out, i)
        return carry

    lax.fori_loop(0, RB, m_rows, 0)

    def y_wait(q, carry):
        got(Y.at[q], yr.at[q])
        return carry

    lax.fori_loop(0, NP, y_wait, 0)

    def gradient(i, carry):
        for s in range(KS):
            b = i * KS + s
            cubic = cub[b] + Y[:, b].reshape(BS, BS).astype(F32)
            direct = pick(accM, i, dcols[i, s:s + 1, :])
            g_out[b] = (3.0 * direct - 2.0 * cubic.T).astype(BF16)
        return carry

    lax.fori_loop(0, RB, gradient, 0)

    for c in sends:
        c.wait_send()

    def drain(q, carry):
        for f, d, half, i, dev in H_OWN + H_MID + H_FAR:
            sent(hp(q, f, d, half), hs.at[q * 9 + i])
        sent(Htw.at[q], ts.at[q])
        for i in range(4):
            sent(Al.at[q, 0], as_.at[q * 4 + i])
            sent(Bl.at[q, 0], bs.at[q * 4 + i])
        sent(Y.at[q], ys.at[q])
        return carry

    lax.fori_loop(0, NP, drain, 0)
    sent(dr(0, 2), cs.at[2])
    sent(dr(1, 2), cs.at[6])


def local(density, density_cols, hamilton, hamilton_cols, filter_cols):
    base = lax.axis_index("col") * CB

    def indicators(cols):
        hit = cols[:, :, None] == base + jnp.arange(CB, dtype=jnp.int32)
        hit = jnp.broadcast_to(hit[..., None], (RB, KS, CB, BS))
        return hit.astype(BF16).reshape(2, IND, BS)

    def places(cols):
        return jnp.broadcast_to((cols - base)[:, :, None], cols.shape + (BS,))

    def values(v):
        return v.reshape(2, HALF, BS)

    hbm = pl.BlockSpec(memory_space=pl.ANY)
    vmem = pl.BlockSpec(memory_space=pltpu.VMEM)
    dma = lambda n: pltpu.SemaphoreType.DMA((n,))
    s, m, g = pl.pallas_call(
        kernel,
        out_shape=(
            jax.ShapeDtypeStruct((RB * CB, BS, BS), BF16),
            jax.ShapeDtypeStruct((RB * CB, BS, BS), BF16),
            jax.ShapeDtypeStruct((RB * KS, BS, BS), BF16),
        ),
        in_specs=[hbm] * 4 + [vmem] * 2,
        out_specs=(vmem,) * 3,
        scratch_shapes=[
            pltpu.VMEM((NR, 2, SH + IND, BS), BF16),
            pltpu.VMEM((NP, NR, 2, 8, JP, BS), BF16),
            pltpu.VMEM((NC, 2, SH, BS), BF16),
            pltpu.VMEM((NP, NR, 8, JP, BS), BF16),
            pltpu.VMEM((NR, IND, BS), BF16),
            pltpu.VMEM((ROWS, COLS), BF16),
            pltpu.VMEM((ROWS, COLS), BF16),
            pltpu.VMEM((NR, ROWS, CHUNK), BF16),
            pltpu.VMEM((CHUNK, COLS), BF16),
            pltpu.VMEM((NR * CB * JP, COLS), BF16),
            pltpu.VMEM((NR * CB * JP, COLS), BF16),
            pltpu.VMEM((ROWS, COLS), F32),
            pltpu.VMEM((ROWS, COLS), F32),
            pltpu.VMEM((3, NR * CB * JP, ROWS), F32),
            pltpu.VMEM((NP, NR, RB * KS, JP, BS), BF16),
            pltpu.VMEM((NP, 2, RB, JP, BS), BF16),
            pltpu.VMEM((NP, 2, RB, JP, BS), BF16),
            pltpu.VMEM((NP, 2, RB * KS, JP, BS), BF16),
            pltpu.VMEM((NP, 2, RB * KS, JP, BS), BF16),
            pltpu.VMEM((NP, RB * KS, JP, BS), BF16),
            pltpu.VMEM((RB * KS, BS, BS), F32),
            dma(5 + NP), dma(10), dma(10), dma(14), dma(14), dma(9 * NP), dma(9 * NP),
            dma(8), dma(8), dma(NP + 2), dma(NP + 2), dma(4 * NP), dma(4 * NP),
            dma(4 * NP), dma(4 * NP), dma(NP), dma(NP),
        ],
        compiler_params=pltpu.CompilerParams(
            collective_id=0, has_side_effects=True, vmem_limit_bytes=67_000_000),
    )(values(density), indicators(density_cols),
      hamilton.reshape(2, 8, NP, JP, BS),
      indicators(hamilton_cols), places(filter_cols), places(density_cols))
    return (s.reshape(RB, CB, BS, BS), m.reshape(RB, CB, BS, BS), g.reshape(RB, KS, BS, BS))


def solution(mesh):
    blocks, cols = P("row", "col", None, None), P("row", "col")
    return jax.shard_map(
        local, mesh=mesh, in_specs=(blocks, cols, blocks, cols, cols),
        out_specs=(blocks,) * 3, check_vma=False)
```

time: 845 us -> 135 us (0.16)
  local copies, waits for them, and re-layouts: 288 us -> 8.48 us
  matrix products: 247 us -> 0 us
  waiting for transfers between devices: 214 us -> 0 us
  Pallas kernels: 0 us -> 126 us
  blocking collectives: 77 us -> 0 us
  between operations: 13.8 us -> 0.69 us
    dot_general x56 -> x0, matrix products: 247 us -> none  [the longest x24 127 us: block_products(): jnp.einsum('sab,stbc->stac', left_vals, chosen, preferred_element_type=jn...]
    all_gather x4 -> x0, waiting for transfers between devices: 211 us -> none  [the longest x1 86.3 us: local(): piece_values = lax.all_gather(square_term, 'col', axis=1, tiled=True)]
    reshape x24 -> x0, local copies, waits for them, and re-layouts: 161 us -> none  [block_products(): block_product_list.reshape(-1, block_size, block_size)]
    pallas_call x0 -> x1, Pallas kernels: none -> 126 us  [local(): pl.pallas_call(kernel, out_shape=(jax.ShapeDtypeStruct((RB * CB, BS, BS),...]
    gather x48 -> x0, local copies, waits for them, and re-layouts: 116 us -> none  [the longest x24 102 us: block_products(): chosen = right_vals[left_cols]]
    all_gather x4 -> x0, blocking collectives: 77 us -> none  [the longest x1 27.3 us: local(): piece_cols = lax.all_gather(density_cols, 'col', axis=1, tiled=True)]
  transfers between devices with their start and end apart: 4 -> 0, of which waited for: 3 -> 0; matrix products, arithmetic and copies ran while one was open for 0% -> 0% of each run, Pallas kernels for 0% -> 0%
where the time goes in v2:
time: 135 us
  Pallas kernels  126 us (93%)
  local copies, waits for them, and re-layouts  8.48 us (6%)
    pallas_call x1, Pallas kernels, local(): pl.pallas_call(kernel, out_shape=(jax.ShapeDtypeStruct((RB * CB, BS, BS),...  126 us
    unnamed x15, local copies, waits for them, and re-layouts  5.42 us

profile of v2, /device:TPU:1, one launch (start us, length us, event | category | flops | bytes accessed | tf_op | source)
XLA Modules:
  0.0 135.0 jit_solution(13516712355468231978)
XLA Ops:
  0.6 0.0 copy-start.2
  0.6 0.0 copy-start.3
  0.7 0.6 copy-done.2
  1.3 0.0 copy-done.3
  1.3 0.1 copy.14
  1.4 0.1 copy.15
  1.5 0.0 copy-start.4
  1.5 0.7 broadcast_in_dim.11.dcols
  2.2 0.0 copy-done.4
  2.2 0.1 copy.13
  2.3 0.1 copy.12
  2.3 0.1 compare_convert_fusion
  2.4 0.1 reshape.51
  2.5 0.1 reshape.50
  2.6 0.7 broadcast_in_dim.10.filt
  3.3 0.7 broadcast_in_dim.8.di
  4.0 0.7 broadcast_in_dim.9.hi
  4.7 125.8 %shard_map.76 = (bf16[32,128,128]{2,1,0:T(8,128)(2,1)}, bf16[32,128,128]{2,1,0:T(8,128)(2,1)}, bf16[16,128,128]{2,1,0:T(8,128)(2,1)}) custom-call(bf16[2,1024,128]{2,1,0:T(8,128)(2,1)} %bitcast.7, bf16[2,32,128]{2,1,0:T(8,128)(2,1)} %broadcast_in_dim.8.di, bf16[2,8,8,16,128]{4,3,2,1,0:T(8,128)(2,1)} %bitcast.8, bf16[2,32,128]{2,1,0:T(8,128)(2,1)} %broadcast_in_dim.9.hi, ...), custom_call_target="tpu_custom_call" | custom-call | tf_op jit(solution)/shard_map/pallas_call | solution.py:476
  130.4 0.0 copy-start
  130.4 2.4 %copy.19 = bf16[8,4,128,128]{3,2,1,0:T(8,128)(2,1)} copy(bf16[8,4,128,128]{3,2,1,0:T(8,128)(2,1)} %bitcast.6) | data formatting | bytes 2097152
  132.8 0.0 copy-done
  132.8 0.0 copy-start.1
  132.8 1.0 copy.20
  133.8 0.4 copy-done.1
  134.2 0.8 copy.21
  (3 shorter events, 0.0 us)
Async XLA Ops:
  0.6 0.7 copy-start.2
  0.6 0.7 copy-start.3
  1.5 0.7 copy-start.4
  130.4 2.4 %copy-start = (bf16[32,128,128]{2,1,0:T(8,128)(2,1)S(1)}, bf16[32,128,128]{2,1,0:T(8,128)(2,1)}, u32[]{:S(2)}) copy-start(bf16[32,128,128]{2,1,0:T(8,128)(2,1)} %get-tuple-element.7) | copy-start | bytes 3145732
  132.8 1.4 %copy-start.1 = (bf16[16,128,128]{2,1,0:T(8,128)(2,1)S(1)}, bf16[16,128,128]{2,1,0:T(8,128)(2,1)}, u32[]{:S(2)}) copy-start(bf16[16,128,128]{2,1,0:T(8,128)(2,1)} %get-tuple-element.8) | copy-start | bytes 1572868

commit v3 on v2

--- a/solution.py
+++ b/solution.py
@@ -28,7 +28,7 @@
 
 def kernel(dv, di, hv, hi, filt, dcols, s_out, m_out, g_out,
            Dcol, Hcol, Drow, Htw, Hti, Sown, Stw, Dd, Rd, Hr0, Hr1, accS, accM, CT,
-           PB, Al, Ar, Bl, Br, Y, cub,
+           PB, OWN, Al, Ar, Bl, Br, Y, cub,
            loc, xs, xr, zs, zr, hs, hr, cs, cr, ts, tr, as_, ar, bs, br, ys, yr):
     row, col = lax.axis_index("row"), lax.axis_index("col")
     x, ylo = row % 4, row // 4
@@ -106,40 +106,15 @@
 
     X(dc(0, 0, 0), 0, ylod)
     X(dc(0, 0, 1), 1, ylod)
-    X(dc(0, 0), 2, xp)
-    X(dc(0, 0), 3, xm)
-    Z(dr(0, 0), 2, zp)
-    Z(dr(0, 0), 3, zm)
+    X(dc(0, 0, 0), 2, xp)
+    X(dc(0, 0, 1), 5, xm)
+    Z(dr(0, 0, 0), 2, zp)
+    Z(dr(0, 0, 1), 5, zm)
+    X(dc(0, 0, 1), 3, xp)
+    X(dc(0, 0, 0), 4, xm)
+    Z(dr(0, 0, 1), 3, zp)
+    Z(dr(0, 0, 0), 4, zm)
     to_twin(0, 0)
-    accS[...] = jnp.zeros_like(accS)
-    accM[...] = jnp.zeros_like(accM)
-    for c in later:
-        c.wait()
-
-    for h in (0, 1):
-        got(dc(1, 0, h), xr.at[h])
-        push(Dcol.at[ridx(1, 0), h, pl.ds(0, SH)], zs.at[h], zr.at[h], yind, Drow.at[col, h])
-    X(dc(1, 0), 4, xp)
-    X(dc(1, 0), 5, xm)
-    got(dc(0, -1), xr.at[2])
-    X(dc(0, -1, 0), 6, xp)
-    got(dc(0, 1), xr.at[3])
-    X(dc(0, 1, 1), 7, xm)
-    got(dr(0, -1), zr.at[2])
-    Z(dr(0, -1, 0), 6, zp)
-    to_twin(0, -1)
-    got(dr(0, 1), zr.at[3])
-    Z(dr(0, 1, 1), 7, zm)
-    to_twin(0, 1)
-    for h in (0, 1):
-        got(dr(1, 0, h), zr.at[h])
-        Z(dr(1, 0, h), 10 + 2 * h, zp)
-        Z(dr(1, 0, h), 11 + 2 * h, zm)
-    to_twin(1, 0)
-    got(dc(1, -1), xr.at[4])
-    X(dc(1, -1, 0), 8, xp)
-    got(dc(1, 1), xr.at[5])
-    X(dc(1, 1, 1), 9, xm)
 
     def hp(q, f, d, half=None):
         k = ridx(f, d)
@@ -178,19 +153,8 @@
         got(hp(q, 1, 2, 0), hr.at[q * 9 + 7])
         got(hp(q, 1, 2, 1), hr.at[q * 9 + 8])
 
-    for q in range(3):
-        h_own(q)
-    got(dr(1, -1, 0), zr.at[10])
-    got(dr(1, -1, 1), zr.at[12])
-    Z(dr(1, -1, 0), 8, zp)
-    to_twin(1, -1)
-    got(dr(1, 1, 0), zr.at[11])
-    got(dr(1, 1, 1), zr.at[13])
-    Z(dr(1, 1, 1), 9, zm)
-    to_twin(1, 1)
-    for f in (0, 1):
-        for d in (0, -1, 1):
-            from_twin(f, d)
+    def h_twin(q):
+        remote(Hcol.at[q, :, 1 - core], Htw.at[q], ts.at[q], tr.at[q], twin).start()
 
     def spread(block, ind, store):
         for ii in range(4):
@@ -217,58 +181,134 @@
     def put_r(at, t, v):
         Rd[at, pl.ds(t * BS, BS)] = v
 
+    def panel(f, d, other):
+        cc = (1 - core) if other else core
+        k = cidx(f, d, other)
+
+        def put(at, t, v):
+            Dd[k // 2, at, pl.ds(pl.multiple_of(cc * COLS + t * BS, BS), BS)] = v
+        spread_d(Drow, k, put)
+
+    def panel2(f, d):
+        from_twin(f, d)
+        panel(f, d, True)
+
+    def chunk(b, f, e):
+        return (1 - ylo if f else ylo) * 4 + (b + e) % 4
+
     dz = (z - x + 4) % 4
     o0 = (dz // 2) * (1 - dz % 2)
     o1 = 1 + 2 * (dz // 2)
     o2 = 4 - o0 - o1
-
-    def order(n):
-        b = n // 2
-        e0 = (1 - b % 2) * (1 - b // 2)
-        e1 = (b % 2) * (1 - b // 2)
-        e2 = (1 - b % 2) * (b // 2)
-        e3 = (b % 2) * (b // 2)
-        return (n % 2) * 4 + (x + e0 * o0 + e1 * o1 + e2 * o2 + e3 * 2 + 4) % 4
-
-    def s_chunk(n, carry):
-        k = order(n)
-        for c in (0, 1):
-            def put(at, t, v, c=c):
-                Dd[k, at, pl.ds(c * COLS + t * BS, BS)] = v
-            spread_d(Drow, 2 * k + c, put)
-        spread_d(Dcol, k, put_r)
-        accS[...] += jnp.dot(Dd[k], Rd[...], preferred_element_type=F32)
-
-        @pl.when(n == 3)
-        def _():
-            got(dr(0, 2, 0), zr.at[6])
-            got(dr(0, 2, 1), zr.at[7])
-            remote(dr(0, 2), dr(0, 2), cs.at[2], cr.at[2], twin).start()
-            for f in (0, 1):
-                got(dc(f, 2, 0), xr.at[6 + 2 * f])
-                got(dc(f, 2, 1), xr.at[7 + 2 * f])
-            h_mid(0)
-            h_mid(1)
-            got(dr(1, 2, 0), zr.at[8])
-            got(dr(1, 2, 1), zr.at[9])
-            remote(dr(1, 2), dr(1, 2), cs.at[6], cr.at[6], twin).start()
-            from_twin(0, 2)
-            from_twin(1, 2)
-
-        @pl.when(n == 5)
-        def _():
-            h_far(0)
-            h_own(3)
-            h_mid(2)
-
-        return carry
-
-    lax.fori_loop(0, 8, s_chunk, 0)
+    odd = (ylo + yhi) % 2
+    plain = [chunk(x, 0, e) for e in range(4)] + [chunk(x, 1, e) for e in (o0, o1, o2, 2)]
+    mixed = [chunk(z, 0, 0), chunk(x, 1, 0), chunk(z, 0, 1), chunk(z, 0, 3),
+             chunk(x, 1, 1), chunk(x, 1, 3), chunk(z, 0, 2), chunk(x, 1, 2)]
+    chunks = [(1 - odd) * a + odd * b for a, b in zip(plain, mixed)]
+
+    def products(n):
+        def body(i, carry):
+            k = chunks[n] + i * (chunks[n + 1] - chunks[n])
+            spread_d(Dcol, k, put_r)
+            accS[...] += jnp.dot(Dd[k], Rd[...], preferred_element_type=F32)
+            return carry
+        lax.fori_loop(0, 2, body, 0)
+
+    accS[...] = jnp.zeros_like(accS)
+    accM[...] = jnp.zeros_like(accM)
+    for c in later:
+        c.wait()
+    panel(0, 0, False)
+
+    def relay(h):
+        got(dc(1, 0, h), xr.at[h])
+        push(Dcol.at[ridx(1, 0), h, pl.ds(0, SH)], zs.at[h], zr.at[h], yind, Drow.at[col, h])
+
+    relay(0)
+    got(dc(0, -1, 0), xr.at[2])
+    X(dc(0, -1, 0), 10, xp)
+    got(dc(0, 1, 1), xr.at[5])
+    X(dc(0, 1, 1), 11, xm)
+    got(dr(0, -1, 0), zr.at[2])
+    Z(dr(0, -1, 0), 10, zp)
+    got(dr(0, 1, 1), zr.at[5])
+    Z(dr(0, 1, 1), 11, zm)
+    panel2(0, 0)
+    relay(1)
+    X(dc(1, 0, 0), 6, xp)
+    X(dc(1, 0, 1), 9, xm)
+    X(dc(1, 0, 1), 7, xp)
+    X(dc(1, 0, 0), 8, xm)
+    got(dr(0, -1, 1), zr.at[3])
+    to_twin(0, -1)
+    got(dr(0, 1, 0), zr.at[4])
+    to_twin(0, 1)
+    panel(0, -1, False)
+    panel(0, 1, False)
+    got(dr(1, 0, 0), zr.at[0])
+    Z(dr(1, 0, 0), 6, zp)
+    Z(dr(1, 0, 0), 8, zm)
+    panel2(0, -1)
+    panel2(0, 1)
+    got(dr(0, 2, 0), zr.at[10])
+    got(dr(0, 2, 1), zr.at[11])
+    to_twin(0, 2)
+    got(dr(1, 0, 1), zr.at[1])
+    Z(dr(1, 0, 1), 7, zp)
+    Z(dr(1, 0, 1), 9, zm)
+    to_twin(1, 0)
+    panel(0, 2, False)
+    panel(1, 0, False)
+    panel2(0, 2)
+    panel2(1, 0)
+    got(dc(0, -1, 1), xr.at[3])
+    got(dc(0, 1, 0), xr.at[4])
+    got(dc(0, 2, 0), xr.at[10])
+    got(dc(0, 2, 1), xr.at[11])
+    products(0)
+    got(dc(1, -1, 0), xr.at[6])
+    X(dc(1, -1, 0), 12, xp)
+    got(dc(1, 1, 1), xr.at[9])
+    X(dc(1, 1, 1), 13, xm)
+    h_own(0)
+    h_own(1)
+    got(dr(1, -1, 0), zr.at[6])
+    Z(dr(1, -1, 0), 12, zp)
+    got(dr(1, 1, 1), zr.at[9])
+    Z(dr(1, 1, 1), 13, zm)
+    got(dr(1, -1, 1), zr.at[7])
+    to_twin(1, -1)
+    got(dr(1, 1, 0), zr.at[8])
+    to_twin(1, 1)
+    panel(1, -1, False)
+    panel(1, 1, False)
+    panel2(1, -1)
+    panel2(1, 1)
+    got(dc(1, -1, 1), xr.at[7])
+    got(dc(1, 1, 0), xr.at[8])
+    products(2)
+    h_own(2)
+    h_mid(0)
+    products(4)
+    got(dr(1, 2, 0), zr.at[12])
+    got(dr(1, 2, 1), zr.at[13])
+    to_twin(1, 2)
+    got(dc(1, 2, 0), xr.at[12])
+    got(dc(1, 2, 1), xr.at[13])
+    h_mid(1)
+    panel(1, 2, False)
+    panel2(1, 2)
+    h_own(3)
+    h_far(0)
+    products(6)
 
     Sown[...] = accS[...].astype(BF16)
     push(Sown, ts.at[NP], tr.at[NP], twin, Stw)
     push(Dcol.at[:, 1 - core, pl.ds(SH, IND)], ts.at[NP + 1], tr.at[NP + 1], twin, Hti)
-    h_far(1)
+    h_mid(2)
+    h_own(4)
+    h_end(0)
+    h_twin(0)
     got(Stw, tr.at[NP])
     got(Hti, tr.at[NP + 1])
 
@@ -298,7 +338,7 @@
             spread(lambda b: Htw[q, m, b], Hti[m].astype(F32), put(Hr1))
             return carry
         lax.fori_loop(0, 8, rows, 0)
-        CT[q % 3] = (
+        CT[q % 2] = (
             lax.dot_general(Hr0[...], Sown[...], NT, preferred_element_type=F32)
             + lax.dot_general(Hr1[...], Stw[...], NT, preferred_element_type=F32)
         )
@@ -307,7 +347,7 @@
         ind = Drow[2 * m + core, half, pl.ds(HALF, IND), :].astype(F32)
         for ii in range(4):
             lanes = pl.ds((half * 4 + ii) * BS, BS)
-            v = [CT[q % 3, pl.ds(pl.multiple_of(m * 64 + t * JP, JP), JP), lanes] for t in range(CB)]
+            v = [CT[q % 2, pl.ds(pl.multiple_of(m * 64 + t * JP, JP), JP), lanes] for t in range(CB)]
             for s in range(KS):
                 out = v[0]
                 for t in range(1, CB):
@@ -344,20 +384,24 @@
                     extract(q, m, half, emit)
                 remote(PB.at[q, m], dst.at[q, f], bs.at[i], br.at[i], dev).start()
 
+    def rs_keep(q):
+        for f in (1, 0):
+            for half in (0, 1):
+                def emit(b, v, half=half):
+                    OWN[q % 3, f, half * 8 + b] = v
+                extract(q, chip(f, 0), half, emit)
+
     def rs_own(q):
         for f in (1, 0):
             m = chip(f, 0)
             got(Bl.at[q, f], br.at[q * 4 + f * 2])
             got(Br.at[q, f], br.at[q * 4 + f * 2 + 1])
-            for half in (0, 1):
-                def emit(b, v, half=half):
-                    b = half * 8 + b
-                    v = v + Bl[q, f, b].astype(F32) + Br[q, f, b].astype(F32)
-                    if f:
-                        PB[q, m, b] = v.astype(BF16)
-                    else:
-                        cub[b, pl.ds(pl.multiple_of(q * JP, JP), JP), :] = v
-                extract(q, m, half, emit)
+            for b in range(RB * KS):
+                v = OWN[q % 3, f, b] + Bl[q, f, b].astype(F32) + Br[q, f, b].astype(F32)
+                if f:
+                    PB[q, m, b] = v.astype(BF16)
+                else:
+                    cub[b, pl.ds(pl.multiple_of(q * JP, JP), JP), :] = v
             if f:
                 remote(PB.at[q, m], Y.at[q], ys.at[q], yr.at[q], yhid).start()
 
@@ -375,22 +419,17 @@
         return carry
 
     def step(q, carry):
-        @pl.when(q < NP)
-        def _():
-            h_end(q)
-            remote(Hcol.at[q, :, 1 - core], Htw.at[q], ts.at[q], tr.at[q], twin).start()
-
-        @pl.when(q + 2 < NP)
-        def _():
-            h_far(q + 2)
+        @pl.when(q + 1 < NP)
+        def _():
+            h_far(q + 1)
 
         @pl.when(q + 3 < NP)
         def _():
             h_mid(q + 3)
 
-        @pl.when(q + 4 < NP)
-        def _():
-            h_own(q + 4)
+        @pl.when(q + 5 < NP)
+        def _():
+            h_own(q + 5)
 
         @pl.when(q < NP)
         def _():
@@ -402,19 +441,25 @@
         @pl.when((q >= 1) & (q < NP + 1))
         def _():
             rs_near(q - 1)
-
-        @pl.when(q >= 2)
-        def _():
-            rs_own(q - 2)
+            rs_keep(q - 1)
+
+        @pl.when(q >= 3)
+        def _():
+            rs_own(q - 3)
+
+        @pl.when(q + 1 < NP)
+        def _():
+            h_end(q + 1)
+            h_twin(q + 1)
 
         @pl.when(q >= NP - 1)
         def _():
-            lo = (q - NP + 1) * 3
-            lax.fori_loop(lo, lo + 3 - (q - NP + 1) // 2, m_chunk, 0)
+            lo = (q - NP + 1) * 2
+            lax.fori_loop(lo, lo + 2, m_chunk, 0)
 
         return carry
 
-    lax.fori_loop(0, NP + 2, step, 0)
+    lax.fori_loop(0, NP + 3, step, 0)
 
     def m_rows(i, carry):
         filtered(accM, m_out, i)
@@ -452,8 +497,6 @@
         return carry
 
     lax.fori_loop(0, NP, drain, 0)
-    sent(dr(0, 2), cs.at[2])
-    sent(dr(1, 2), cs.at[6])
 
 
 def local(density, density_cols, hamilton, hamilton_cols, filter_cols):
@@ -496,15 +539,16 @@
             pltpu.VMEM((NR * CB * JP, COLS), BF16),
             pltpu.VMEM((ROWS, COLS), F32),
             pltpu.VMEM((ROWS, COLS), F32),
-            pltpu.VMEM((3, NR * CB * JP, ROWS), F32),
+            pltpu.VMEM((2, NR * CB * JP, ROWS), F32),
             pltpu.VMEM((NP, NR, RB * KS, JP, BS), BF16),
+            pltpu.VMEM((3, 2, RB * KS, JP, BS), F32),
             pltpu.VMEM((NP, 2, RB, JP, BS), BF16),
             pltpu.VMEM((NP, 2, RB, JP, BS), BF16),
             pltpu.VMEM((NP, 2, RB * KS, JP, BS), BF16),
             pltpu.VMEM((NP, 2, RB * KS, JP, BS), BF16),
             pltpu.VMEM((NP, RB * KS, JP, BS), BF16),
             pltpu.VMEM((RB * KS, BS, BS), F32),
-            dma(5 + NP), dma(10), dma(10), dma(14), dma(14), dma(9 * NP), dma(9 * NP),
+            dma(5 + NP), dma(14), dma(14), dma(14), dma(14), dma(9 * NP), dma(9 * NP),
             dma(8), dma(8), dma(NP + 2), dma(NP + 2), dma(4 * NP), dma(4 * NP),
             dma(4 * NP), dma(4 * NP), dma(NP), dma(NP),
         ],

time: 135 us -> 123 us (0.911)
  Pallas kernels: 126 us -> 113 us
    pallas_call x1, Pallas kernels: 126 us -> 113 us  [local(): pl.pallas_call(kernel, out_shape=(jax.ShapeDtypeStruct((RB * CB, BS, BS),...]
where the time goes in v3:
time: 123 us; the launch traced here: 122 us
  Pallas kernels  113 us (92%)
  local copies, waits for them, and re-layouts  8.48 us (7%)
    pallas_call x1, Pallas kernels, local(): pl.pallas_call(kernel, out_shape=(jax.ShapeDtypeStruct((RB * CB, BS, BS),...  113 us
    unnamed x15, local copies, waits for them, and re-layouts  5.42 us

profile of v3, /device:TPU:1, one launch (start us, length us, event | category | flops | bytes accessed | tf_op | source)
XLA Modules:
  0.0 122.2 jit_solution(17602453387935718809)
XLA Ops:
  0.6 0.0 copy-start.2
  0.6 0.0 copy-start.3
  0.7 0.6 copy-done.2
  1.3 0.0 copy-done.3
  1.3 0.1 copy.14
  1.4 0.1 copy.15
  1.5 0.0 copy-start.4
  1.5 0.7 broadcast_in_dim.11.dcols
  2.2 0.0 copy-done.4
  2.2 0.1 copy.13
  2.3 0.1 copy.12
  2.3 0.1 compare_convert_fusion
  2.4 0.1 reshape.51
  2.5 0.1 reshape.50
  2.6 0.7 broadcast_in_dim.10.filt
  3.3 0.7 broadcast_in_dim.8.di
  4.0 0.7 broadcast_in_dim.9.hi
  4.7 112.9 %shard_map.76 = (bf16[32,128,128]{2,1,0:T(8,128)(2,1)}, bf16[32,128,128]{2,1,0:T(8,128)(2,1)}, bf16[16,128,128]{2,1,0:T(8,128)(2,1)}) custom-call(bf16[2,1024,128]{2,1,0:T(8,128)(2,1)} %bitcast.7, bf16[2,32,128]{2,1,0:T(8,128)(2,1)} %broadcast_in_dim.8.di, bf16[2,8,8,16,128]{4,3,2,1,0:T(8,128)(2,1)} %bitcast.8, bf16[2,32,128]{2,1,0:T(8,128)(2,1)} %broadcast_in_dim.9.hi, ...), custom_call_target="tpu_custom_call" | custom-call | tf_op jit(solution)/shard_map/pallas_call | solution.py:519
  117.6 0.0 copy-start
  117.6 2.4 %copy.19 = bf16[8,4,128,128]{3,2,1,0:T(8,128)(2,1)} copy(bf16[8,4,128,128]{3,2,1,0:T(8,128)(2,1)} %bitcast.6) | data formatting | bytes 2097152
  120.0 0.0 copy-done
  120.0 0.0 copy-start.1
  120.0 1.0 copy.20
  121.0 0.4 copy-done.1
  121.4 0.8 copy.21
  (3 shorter events, 0.0 us)
Async XLA Ops:
  0.6 0.7 copy-start.2
  0.6 0.7 copy-start.3
  1.5 0.7 copy-start.4
  117.6 2.4 %copy-start = (bf16[32,128,128]{2,1,0:T(8,128)(2,1)S(1)}, bf16[32,128,128]{2,1,0:T(8,128)(2,1)}, u32[]{:S(2)}) copy-start(bf16[32,128,128]{2,1,0:T(8,128)(2,1)} %get-tuple-element.7) | copy-start | bytes 3145732
  120.0 1.4 %copy-start.1 = (bf16[16,128,128]{2,1,0:T(8,128)(2,1)S(1)}, bf16[16,128,128]{2,1,0:T(8,128)(2,1)}, u32[]{:S(2)}) copy-start(bf16[16,128,128]{2,1,0:T(8,128)(2,1)} %get-tuple-element.8) | copy-start | bytes 1572868

commit v4 on v3

--- a/solution.py
+++ b/solution.py
@@ -16,6 +16,7 @@
 SH = HALF + IND
 NP = 8
 JP = BS // NP
+HS = 8
 ROWS, COLS, CHUNK = RB * BS, CB * BS, RB * BS
 
 
@@ -26,8 +27,8 @@
     )
 
 
-def kernel(dv, di, hv, hi, filt, dcols, s_out, m_out, g_out,
-           Dcol, Hcol, Drow, Htw, Hti, Sown, Stw, Dd, Rd, Hr0, Hr1, accS, accM, CT,
+def kernel(dv, hv, dcols, hcols, s_out, m_out, g_out,
+           Dcol, Hcol, Drow, Htw, Hti, Sown, Stw, Mout, Dd, Rd, Hr0, Hr1, accS, accM, CT,
            PB, OWN, Al, Ar, Bl, Br, Y, cub,
            loc, xs, xr, zs, zr, hs, hr, cs, cr, ts, tr, as_, ar, bs, br, ys, yr):
     row, col = lax.axis_index("row"), lax.axis_index("col")
@@ -52,13 +53,10 @@
 
     first = [
         pltpu.make_async_copy(dv, Dcol.at[row, :, pl.ds(0, HALF), :], loc.at[0]),
-        pltpu.make_async_copy(di, Dcol.at[row, :, pl.ds(HALF, IND), :], loc.at[1]),
-        pltpu.make_async_copy(hi, Dcol.at[row, :, pl.ds(SH, IND), :], loc.at[2]),
-        pltpu.make_async_copy(dv, Drow.at[col, :, pl.ds(0, HALF), :], loc.at[3]),
-        pltpu.make_async_copy(di, Drow.at[col, :, pl.ds(HALF, IND), :], loc.at[4]),
+        pltpu.make_async_copy(dv, Drow.at[col, :, pl.ds(0, HALF), :], loc.at[1]),
     ]
     later = [
-        pltpu.make_async_copy(hv.at[:, :, q], Hcol.at[q, row], loc.at[5 + q])
+        pltpu.make_async_copy(hv.at[:, :, q], Hcol.at[q, row], loc.at[2 + q])
         for q in range(NP)
     ]
     for c in first + later:
@@ -66,6 +64,22 @@
     barrier = pltpu.get_barrier_semaphore()
     for dev in (xp, xm, zp, zm, ylod, yind, yhid, twin):
         pl.semaphore_signal(barrier, inc=1, device_id=dev, device_id_type=MESH)
+
+    line = lax.broadcasted_iota(jnp.int32, (IND, BS), 0)
+
+    def indicators(cols, half):
+        place = jnp.zeros((IND, BS), jnp.int32)
+        for ii in range(4):
+            for s in range(KS):
+                c = jnp.full((IND, BS), cols[half * 4 + ii, s] - col * CB, jnp.int32)
+                place = jnp.where(line // CB == ii * KS + s, c, place)
+        return jnp.where(place == line % CB, 1.0, 0.0).astype(BF16)
+
+    for half in (0, 1):
+        ind = indicators(dcols, half)
+        Dcol[row, half, pl.ds(HALF, IND), :] = ind
+        Drow[col, half, pl.ds(HALF, IND), :] = ind
+        Dcol[row, half, pl.ds(SH, IND), :] = indicators(hcols, half)
     for c in first:
         c.wait()
     pl.semaphore_wait(barrier, 8)
@@ -90,6 +104,9 @@
     def dr(f, d, half=None, other=False):
         k = cidx(f, d, other)
         return Drow.at[k] if half is None else Drow.at[k, half]
+
+    def quarter(f, d, part):
+        return Drow.at[cidx(f, d), 0, pl.ds(part * (SH // 2), SH // 2)]
 
     def X(view, i, dev):
         push(view, xs.at[i], xr.at[i], dev)
@@ -121,37 +138,35 @@
         return Hcol.at[q, k] if half is None else Hcol.at[q, k, half]
 
     H_OWN = ((0, 0, None, 0, ylod), (0, 0, None, 1, xp), (0, 0, None, 2, xm))
-    H_MID = ((1, 0, None, 3, xp), (1, 0, None, 4, xm), (0, -1, 0, 5, xp), (0, 1, 1, 6, xm))
-    H_FAR = ((1, -1, 0, 7, xp), (1, 1, 1, 8, xm))
+    H_MID = ((0, -1, 0, 5, xp), (0, 1, 1, 6, xm), (1, 0, None, 3, xp), (1, 0, None, 4, xm))
+    H_FAR = ((0, 2, None, 7, ylod),)
 
     def h_push(q, f, d, half, i, dev):
         view = hp(q, f, d, half)
-        remote(view, view, hs.at[q * 9 + i], hr.at[q * 9 + i], dev).start()
+        remote(view, view, hs.at[q * HS + i], hr.at[q * HS + i], dev).start()
 
     def h_own(q):
         for a in H_OWN:
             h_push(q, *a)
 
     def h_mid(q):
-        got(hp(q, 1, 0), hr.at[q * 9])
+        got(hp(q, 0, -1), hr.at[q * HS + 1])
         h_push(q, *H_MID[0])
+        got(hp(q, 0, 1), hr.at[q * HS + 2])
         h_push(q, *H_MID[1])
-        got(hp(q, 0, -1), hr.at[q * 9 + 1])
+        got(hp(q, 1, 0), hr.at[q * HS])
         h_push(q, *H_MID[2])
-        got(hp(q, 0, 1), hr.at[q * 9 + 2])
         h_push(q, *H_MID[3])
 
     def h_far(q):
-        got(hp(q, 1, -1), hr.at[q * 9 + 3])
+        got(hp(q, 0, 2, 0), hr.at[q * HS + 5])
+        got(hp(q, 0, 2, 1), hr.at[q * HS + 6])
         h_push(q, *H_FAR[0])
-        got(hp(q, 1, 1), hr.at[q * 9 + 4])
-        h_push(q, *H_FAR[1])
 
     def h_end(q):
-        got(hp(q, 0, 2, 0), hr.at[q * 9 + 5])
-        got(hp(q, 0, 2, 1), hr.at[q * 9 + 6])
-        got(hp(q, 1, 2, 0), hr.at[q * 9 + 7])
-        got(hp(q, 1, 2, 1), hr.at[q * 9 + 8])
+        got(hp(q, 1, -1), hr.at[q * HS + 3])
+        got(hp(q, 1, 1), hr.at[q * HS + 4])
+        got(hp(q, 1, 2), hr.at[q * HS + 7])
 
     def h_twin(q):
         remote(Hcol.at[q, :, 1 - core], Htw.at[q], ts.at[q], tr.at[q], twin).start()
@@ -201,16 +216,18 @@
     o1 = 1 + 2 * (dz // 2)
     o2 = 4 - o0 - o1
     odd = (ylo + yhi) % 2
-    plain = [chunk(x, 0, e) for e in range(4)] + [chunk(x, 1, e) for e in (o0, o1, o2, 2)]
+    plain = [chunk(x, 0, e) for e in range(4)] + [chunk(x, 1, e) for e in (o0, o1, o2 + 2 - (dz + 2) % 4, (dz + 2) % 4)]
     mixed = [chunk(z, 0, 0), chunk(x, 1, 0), chunk(z, 0, 1), chunk(z, 0, 3),
-             chunk(x, 1, 1), chunk(x, 1, 3), chunk(z, 0, 2), chunk(x, 1, 2)]
+             chunk(x, 1, 1), chunk(x, 1, 3), chunk(x, 1, 2), chunk(z, 0, 2)]
     chunks = [(1 - odd) * a + odd * b for a, b in zip(plain, mixed)]
+
+    def product(k):
+        spread_d(Dcol, k, put_r)
+        accS[...] += jnp.dot(Dd[k], Rd[...], preferred_element_type=F32)
 
     def products(n):
         def body(i, carry):
-            k = chunks[n] + i * (chunks[n + 1] - chunks[n])
-            spread_d(Dcol, k, put_r)
-            accS[...] += jnp.dot(Dd[k], Rd[...], preferred_element_type=F32)
+            product(chunks[n] + i * (chunks[n + 1] - chunks[n]))
             return carry
         lax.fori_loop(0, 2, body, 0)
 
@@ -239,6 +256,9 @@
     X(dc(1, 0, 1), 9, xm)
     X(dc(1, 0, 1), 7, xp)
     X(dc(1, 0, 0), 8, xm)
+    h_own(0)
+    h_own(1)
+    h_own(2)
     got(dr(0, -1, 1), zr.at[3])
     to_twin(0, -1)
     got(dr(0, 1, 0), zr.at[4])
@@ -250,8 +270,13 @@
     Z(dr(1, 0, 0), 8, zm)
     panel2(0, -1)
     panel2(0, 1)
+    got(dc(0, 2, 0), xr.at[10])
+    X(dc(0, 2, 0), 12, ylod)
+    got(dc(0, 2, 1), xr.at[11])
+    X(dc(0, 2, 1), 13, ylod)
     got(dr(0, 2, 0), zr.at[10])
     got(dr(0, 2, 1), zr.at[11])
+    Z(dr(0, 2, 1), 14, yhid)
     to_twin(0, 2)
     got(dr(1, 0, 1), zr.at[1])
     Z(dr(1, 0, 1), 7, zp)
@@ -263,66 +288,60 @@
     panel2(1, 0)
     got(dc(0, -1, 1), xr.at[3])
     got(dc(0, 1, 0), xr.at[4])
-    got(dc(0, 2, 0), xr.at[10])
-    got(dc(0, 2, 1), xr.at[11])
     products(0)
-    got(dc(1, -1, 0), xr.at[6])
-    X(dc(1, -1, 0), 12, xp)
-    got(dc(1, 1, 1), xr.at[9])
-    X(dc(1, 1, 1), 13, xm)
-    h_own(0)
-    h_own(1)
     got(dr(1, -1, 0), zr.at[6])
-    Z(dr(1, -1, 0), 12, zp)
-    got(dr(1, 1, 1), zr.at[9])
-    Z(dr(1, 1, 1), 13, zm)
+    Z(quarter(1, -1, 0), 12, zp)
+    got(dr(1, 1, 0), zr.at[8])
+    Z(quarter(1, 1, 1), 13, zm)
     got(dr(1, -1, 1), zr.at[7])
     to_twin(1, -1)
-    got(dr(1, 1, 0), zr.at[8])
+    got(dr(1, 1, 1), zr.at[9])
     to_twin(1, 1)
     panel(1, -1, False)
     panel(1, 1, False)
     panel2(1, -1)
     panel2(1, 1)
+    got(dc(1, -1, 0), xr.at[6])
+    got(dc(1, 1, 1), xr.at[9])
     got(dc(1, -1, 1), xr.at[7])
     got(dc(1, 1, 0), xr.at[8])
     products(2)
-    h_own(2)
     h_mid(0)
+    h_own(3)
     products(4)
-    got(dr(1, 2, 0), zr.at[12])
-    got(dr(1, 2, 1), zr.at[13])
-    to_twin(1, 2)
     got(dc(1, 2, 0), xr.at[12])
     got(dc(1, 2, 1), xr.at[13])
+    push(Dcol.at[:, 1 - core, pl.ds(SH, IND)], ts.at[NP + 1], tr.at[NP + 1], twin, Hti)
+    got(quarter(1, 2, 0), zr.at[12])
+    got(quarter(1, 2, 1), zr.at[13])
+    got(dr(1, 2, 1), zr.at[14])
+    to_twin(1, 2)
     h_mid(1)
+    h_far(0)
+    h_own(4)
+    product(chunks[6])
     panel(1, 2, False)
     panel2(1, 2)
-    h_own(3)
-    h_far(0)
-    products(6)
+    product(chunks[7])
 
     Sown[...] = accS[...].astype(BF16)
     push(Sown, ts.at[NP], tr.at[NP], twin, Stw)
-    push(Dcol.at[:, 1 - core, pl.ds(SH, IND)], ts.at[NP + 1], tr.at[NP + 1], twin, Hti)
     h_mid(2)
-    h_own(4)
+    h_far(1)
+    h_own(5)
     h_end(0)
     h_twin(0)
-    got(Stw, tr.at[NP])
+    out_s = pltpu.make_async_copy(Sown, s_out, loc.at[0])
+    out_s.start()
     got(Hti, tr.at[NP + 1])
 
     def pick(acc, i, which):
         at = pl.ds(pl.multiple_of(i * BS, BS), BS)
-        place = jnp.broadcast_to(which, (BS, BS))
+        place = jnp.full((BS, BS), which, jnp.int32)
         out = acc[at, pl.ds(0, BS)]
         for t in range(1, CB):
             out = jnp.where(place == t, acc[at, pl.ds(t * BS, BS)], out)
         return out
-
-    def filtered(acc, out, i):
-        for w in range(CB):
-            out[i * CB + w] = pick(acc, i, filt[i, w:w + 1, :]).astype(BF16)
 
     NT = (((1,), (1,)), ((), ()))
 
@@ -338,6 +357,11 @@
             spread(lambda b: Htw[q, m, b], Hti[m].astype(F32), put(Hr1))
             return carry
         lax.fori_loop(0, 8, rows, 0)
+
+        @pl.when(q == 0)
+        def _():
+            got(Stw, tr.at[NP])
+
         CT[q % 2] = (
             lax.dot_general(Hr0[...], Sown[...], NT, preferred_element_type=F32)
             + lax.dot_general(Hr1[...], Stw[...], NT, preferred_element_type=F32)
@@ -419,21 +443,20 @@
         return carry
 
     def step(q, carry):
-        @pl.when(q + 1 < NP)
-        def _():
-            h_far(q + 1)
+        @pl.when(q + 2 < NP)
+        def _():
+            h_far(q + 2)
 
         @pl.when(q + 3 < NP)
         def _():
             h_mid(q + 3)
 
-        @pl.when(q + 5 < NP)
-        def _():
-            h_own(q + 5)
+        @pl.when(q + 6 < NP)
+        def _():
+            h_own(q + 6)
 
         @pl.when(q < NP)
         def _():
-            filtered(accS, s_out, q)
             got(Htw.at[q], tr.at[q])
             partials(q)
             rs_far(q)
@@ -461,11 +484,9 @@
 
     lax.fori_loop(0, NP + 3, step, 0)
 
-    def m_rows(i, carry):
-        filtered(accM, m_out, i)
-        return carry
-
-    lax.fori_loop(0, RB, m_rows, 0)
+    Mout[...] = accM[...].astype(BF16)
+    out_m = pltpu.make_async_copy(Mout, m_out, loc.at[1])
+    out_m.start()
 
     def y_wait(q, carry):
         got(Y.at[q], yr.at[q])
@@ -477,18 +498,20 @@
         for s in range(KS):
             b = i * KS + s
             cubic = cub[b] + Y[:, b].reshape(BS, BS).astype(F32)
-            direct = pick(accM, i, dcols[i, s:s + 1, :])
+            direct = pick(accM, i, dcols[i, s] - col * CB)
             g_out[b] = (3.0 * direct - 2.0 * cubic.T).astype(BF16)
         return carry
 
     lax.fori_loop(0, RB, gradient, 0)
+    out_s.wait()
+    out_m.wait()
 
     for c in sends:
         c.wait_send()
 
     def drain(q, carry):
         for f, d, half, i, dev in H_OWN + H_MID + H_FAR:
-            sent(hp(q, f, d, half), hs.at[q * 9 + i])
+            sent(hp(q, f, d, half), hs.at[q * HS + i])
         sent(Htw.at[q], ts.at[q])
         for i in range(4):
             sent(Al.at[q, 0], as_.at[q * 4 + i])
@@ -499,38 +522,51 @@
     lax.fori_loop(0, NP, drain, 0)
 
 
+def place_kernel(filt, s_in, m_in, g_in, s_out, m_out, g_out, sv, mv, gv, came, went):
+    base = lax.axis_index("col") * CB
+    ins = [pltpu.make_async_copy(a, v, came.at[n])
+           for n, (a, v) in enumerate(((s_in, sv), (m_in, mv), (g_in, gv)))]
+    for c in ins:
+        c.start()
+    outs = []
+    for n, (v, out) in enumerate(((sv, s_out), (mv, m_out))):
+        ins[n].wait()
+        for i in range(RB):
+            for w in range(CB):
+                lanes = pl.ds(pl.multiple_of((filt[i, w] - base) * BS, BS), BS)
+                k = i * CB + w
+                c = pltpu.make_async_copy(
+                    v.at[pl.ds(i * BS, BS), lanes], out.at[k], went.at[n * RB * CB + k])
+                c.start()
+                outs.append(c)
+    ins[2].wait()
+    c = pltpu.make_async_copy(gv, g_out, went.at[2 * RB * CB])
+    c.start()
+    for c in outs + [c]:
+        c.wait()
+
+
 def local(density, density_cols, hamilton, hamilton_cols, filter_cols):
-    base = lax.axis_index("col") * CB
-
-    def indicators(cols):
-        hit = cols[:, :, None] == base + jnp.arange(CB, dtype=jnp.int32)
-        hit = jnp.broadcast_to(hit[..., None], (RB, KS, CB, BS))
-        return hit.astype(BF16).reshape(2, IND, BS)
-
-    def places(cols):
-        return jnp.broadcast_to((cols - base)[:, :, None], cols.shape + (BS,))
-
-    def values(v):
-        return v.reshape(2, HALF, BS)
-
     hbm = pl.BlockSpec(memory_space=pl.ANY)
     vmem = pl.BlockSpec(memory_space=pltpu.VMEM)
+    smem = pl.BlockSpec(memory_space=pltpu.SMEM)
     dma = lambda n: pltpu.SemaphoreType.DMA((n,))
     s, m, g = pl.pallas_call(
         kernel,
         out_shape=(
-            jax.ShapeDtypeStruct((RB * CB, BS, BS), BF16),
-            jax.ShapeDtypeStruct((RB * CB, BS, BS), BF16),
+            jax.ShapeDtypeStruct((ROWS, COLS), BF16),
+            jax.ShapeDtypeStruct((ROWS, COLS), BF16),
             jax.ShapeDtypeStruct((RB * KS, BS, BS), BF16),
         ),
-        in_specs=[hbm] * 4 + [vmem] * 2,
-        out_specs=(vmem,) * 3,
+        in_specs=[hbm] * 2 + [smem] * 2,
+        out_specs=(hbm, hbm, vmem),
         scratch_shapes=[
             pltpu.VMEM((NR, 2, SH + IND, BS), BF16),
             pltpu.VMEM((NP, NR, 2, 8, JP, BS), BF16),
             pltpu.VMEM((NC, 2, SH, BS), BF16),
             pltpu.VMEM((NP, NR, 8, JP, BS), BF16),
             pltpu.VMEM((NR, IND, BS), BF16),
+            pltpu.VMEM((ROWS, COLS), BF16),
             pltpu.VMEM((ROWS, COLS), BF16),
             pltpu.VMEM((ROWS, COLS), BF16),
             pltpu.VMEM((NR, ROWS, CHUNK), BF16),
@@ -548,15 +584,26 @@
             pltpu.VMEM((NP, 2, RB * KS, JP, BS), BF16),
             pltpu.VMEM((NP, RB * KS, JP, BS), BF16),
             pltpu.VMEM((RB * KS, BS, BS), F32),
-            dma(5 + NP), dma(14), dma(14), dma(14), dma(14), dma(9 * NP), dma(9 * NP),
+            dma(2 + NP), dma(14), dma(14), dma(15), dma(15), dma(HS * NP), dma(HS * NP),
             dma(8), dma(8), dma(NP + 2), dma(NP + 2), dma(4 * NP), dma(4 * NP),
             dma(4 * NP), dma(4 * NP), dma(NP), dma(NP),
         ],
         compiler_params=pltpu.CompilerParams(
             collective_id=0, has_side_effects=True, vmem_limit_bytes=67_000_000),
-    )(values(density), indicators(density_cols),
-      hamilton.reshape(2, 8, NP, JP, BS),
-      indicators(hamilton_cols), places(filter_cols), places(density_cols))
+    )(density.reshape(2, HALF, BS), hamilton.reshape(2, 8, NP, JP, BS), density_cols, hamilton_cols)
+    slots = jax.ShapeDtypeStruct((RB * CB, BS, BS), BF16)
+    s, m, g = pl.pallas_call(
+        place_kernel,
+        out_shape=(slots, slots, jax.ShapeDtypeStruct((RB * KS, BS, BS), BF16)),
+        in_specs=[smem] + [hbm] * 3,
+        out_specs=(hbm,) * 3,
+        scratch_shapes=[
+            pltpu.VMEM((ROWS, COLS), BF16),
+            pltpu.VMEM((ROWS, COLS), BF16),
+            pltpu.VMEM((RB * KS, BS, BS), BF16),
+            dma(3), dma(2 * RB * CB + 1),
+        ],
+    )(filter_cols, s, m, g)
     return (s.reshape(RB, CB, BS, BS), m.reshape(RB, CB, BS, BS), g.reshape(RB, KS, BS, BS))
 
 

time: 123 us -> 116 us (0.943)
  local copies, waits for them, and re-layouts: 8.48 us -> 2.7 us
    unnamed x15 -> x9, local copies, waits for them, and re-layouts: 5.42 us -> 2.7 us
    broadcast_in_dim x4 -> x0, local copies, waits for them, and re-layouts: 2.72 us -> none  [the longest x2 1.36 us: indicators(): hit = jnp.broadcast_to(hit[..., None], (RB, KS, CB, BS))]
    pallas_call x1 -> x2, Pallas kernels: 113 us -> 112 us  [the longest x1 108 us: local(): pl.pallas_call(kernel, out_shape=(jax.ShapeDtypeStruct((ROWS, COLS), BF16...]
where the time goes in v4:
time: 116 us; the launch traced here: 115 us
  Pallas kernels  112 us (97%)
  local copies, waits for them, and re-layouts  2.7 us (2%)
    pallas_call x1, Pallas kernels, local(): pl.pallas_call(kernel, out_shape=(jax.ShapeDtypeStruct((ROWS, COLS), BF16...  108 us
    pallas_call x1, Pallas kernels, local(): pl.pallas_call(place_kernel, out_shape=(slots, slots, jax.ShapeDtypeStruc...  4.02 us
    unnamed x9, local copies, waits for them, and re-layouts  2.7 us

profile of v4, /device:TPU:1, one launch (start us, length us, event | category | flops | bytes accessed | tf_op | source)
XLA Modules:
  0.0 115.4 jit_solution(17592845329595250839)
XLA Ops:
  0.6 0.0 copy-start.1
  0.6 0.7 copy-done.1
  1.3 0.0 copy-start.2
  1.3 0.7 copy.8.dcols
  2.0 0.0 copy-done.2
  2.0 0.0 copy-start
  2.0 0.7 copy.9.hcols
  2.7 0.0 copy-done
  2.7 0.7 copy.10.filt
  3.3 108.0 %shard_map.76 = (bf16[1024,512]{1,0:T(8,128)(2,1)}, bf16[1024,512]{1,0:T(8,128)(2,1)}, bf16[16,128,128]{2,1,0:T(8,128)(2,1)}) custom-call(bf16[2,1024,128]{2,1,0:T(8,128)(2,1)} %bitcast.5, bf16[2,8,8,16,128]{4,3,2,1,0:T(8,128)(2,1)} %bitcast.6, s32[8,2]{1,0:T(8,128)} %copy.8.dcols, s32[8,2]{1,0:T(8,128)} %copy.9.hcols), custom_call_target="tpu_custom_call" | custom-call | tf_op jit(solution)/shard_map/pallas_call | solution.py:554
  111.3 4.0 %shard_map.77 = (bf16[32,128,128]{2,1,0:T(8,128)(2,1)}, bf16[32,128,128]{2,1,0:T(8,128)(2,1)}, bf16[16,128,128]{2,1,0:T(8,128)(2,1)}) custom-call(s32[8,4]{1,0:T(8,128)} %copy.10.filt, bf16[1024,512]{1,0:T(8,128)(2,1)} %get-tuple-element.9.s_in, bf16[1024,512]{1,0:T(8,128)(2,1)} %get-tuple-element.10.m_in, bf16[16,128,128]{2,1,0:T(8,128)(2,1)} %get-tuple-element.11.g_in), custom_call_target="tpu_custom_call" | custom-call | tf_op jit(solution)/shard_map/pallas_call | solution.py:595
Async XLA Ops:
  0.6 0.7 copy-start.1
  1.3 0.7 copy-start.2
  2.0 0.7 copy-start

commit v5 on v4

--- a/solution.py
+++ b/solution.py
@@ -71,7 +71,7 @@
         place = jnp.zeros((IND, BS), jnp.int32)
         for ii in range(4):
             for s in range(KS):
-                c = jnp.full((IND, BS), cols[half * 4 + ii, s] - col * CB, jnp.int32)
+                c = jnp.full((IND, BS), cols[s, half * 4 + ii] - col * CB, jnp.int32)
                 place = jnp.where(line // CB == ii * KS + s, c, place)
         return jnp.where(place == line % CB, 1.0, 0.0).astype(BF16)
 
@@ -104,9 +104,6 @@
     def dr(f, d, half=None, other=False):
         k = cidx(f, d, other)
         return Drow.at[k] if half is None else Drow.at[k, half]
-
-    def quarter(f, d, part):
-        return Drow.at[cidx(f, d), 0, pl.ds(part * (SH // 2), SH // 2)]
 
     def X(view, i, dev):
         push(view, xs.at[i], xr.at[i], dev)
@@ -276,7 +273,6 @@
     X(dc(0, 2, 1), 13, ylod)
     got(dr(0, 2, 0), zr.at[10])
     got(dr(0, 2, 1), zr.at[11])
-    Z(dr(0, 2, 1), 14, yhid)
     to_twin(0, 2)
     got(dr(1, 0, 1), zr.at[1])
     Z(dr(1, 0, 1), 7, zp)
@@ -290,12 +286,12 @@
     got(dc(0, 1, 0), xr.at[4])
     products(0)
     got(dr(1, -1, 0), zr.at[6])
-    Z(quarter(1, -1, 0), 12, zp)
-    got(dr(1, 1, 0), zr.at[8])
-    Z(quarter(1, 1, 1), 13, zm)
+    Z(dr(1, -1, 0), 12, zp)
+    got(dr(1, 1, 1), zr.at[9])
+    Z(dr(1, 1, 1), 13, zm)
     got(dr(1, -1, 1), zr.at[7])
     to_twin(1, -1)
-    got(dr(1, 1, 1), zr.at[9])
+    got(dr(1, 1, 0), zr.at[8])
     to_twin(1, 1)
     panel(1, -1, False)
     panel(1, 1, False)
@@ -312,9 +308,8 @@
     got(dc(1, 2, 0), xr.at[12])
     got(dc(1, 2, 1), xr.at[13])
     push(Dcol.at[:, 1 - core, pl.ds(SH, IND)], ts.at[NP + 1], tr.at[NP + 1], twin, Hti)
-    got(quarter(1, 2, 0), zr.at[12])
-    got(quarter(1, 2, 1), zr.at[13])
-    got(dr(1, 2, 1), zr.at[14])
+    got(dr(1, 2, 0), zr.at[12])
+    got(dr(1, 2, 1), zr.at[13])
     to_twin(1, 2)
     h_mid(1)
     h_far(0)
@@ -429,7 +424,7 @@
             if f:
                 remote(PB.at[q, m], Y.at[q], ys.at[q], yr.at[q], yhid).start()
 
-    def m_chunk(k, carry):
+    def m_chunk(k):
         def body(half, c):
             ind = Dcol[k, half, pl.ds(SH, IND), :].astype(F32)
 
@@ -440,7 +435,12 @@
             return c
         lax.fori_loop(0, 2, body, 0)
         accM[...] += jnp.dot(Dd[k], Rd[...], preferred_element_type=F32)
-        return carry
+
+    def m_order(n):
+        m, late = n % 4, n // 4
+        f = (1 - late) * (m * (3 - m) * (2 - m) // 2) + late * (1 - (m // 2) * (1 - m % 2))
+        d = (1 - late) * ((m // 2) * (2 * m - 3)) + late * ((1 - m // 2) * (1 + 2 * m) + 2 * (m // 2))
+        return ((ylo + f) % 2) * 4 + (x + d + 4) % 4
 
     def step(q, carry):
         @pl.when(q + 2 < NP)
@@ -475,34 +475,38 @@
             h_end(q + 1)
             h_twin(q + 1)
 
-        @pl.when(q >= NP - 1)
-        def _():
-            lo = (q - NP + 1) * 2
-            lax.fori_loop(lo, lo + 2, m_chunk, 0)
+        @pl.when(q >= NP - 4)
+        def _():
+            m_chunk(m_order(q - NP + 4))
 
         return carry
 
     lax.fori_loop(0, NP + 3, step, 0)
+    m_chunk(m_order(7))
 
     Mout[...] = accM[...].astype(BF16)
     out_m = pltpu.make_async_copy(Mout, m_out, loc.at[1])
     out_m.start()
 
+    def direct(i, carry):
+        for s in range(KS):
+            b = i * KS + s
+            cub[b] = 3.0 * pick(accM, i, dcols[s, i] - col * CB) - 2.0 * cub[b].T
+        return carry
+
+    lax.fori_loop(0, RB, direct, 0)
+
     def y_wait(q, carry):
         got(Y.at[q], yr.at[q])
         return carry
 
     lax.fori_loop(0, NP, y_wait, 0)
 
-    def gradient(i, carry):
-        for s in range(KS):
-            b = i * KS + s
-            cubic = cub[b] + Y[:, b].reshape(BS, BS).astype(F32)
-            direct = pick(accM, i, dcols[i, s] - col * CB)
-            g_out[b] = (3.0 * direct - 2.0 * cubic.T).astype(BF16)
+    def gradient(b, carry):
+        g_out[b] = (cub[b] - 2.0 * Y[:, b].reshape(BS, BS).astype(F32).T).astype(BF16)
         return carry
 
-    lax.fori_loop(0, RB, gradient, 0)
+    lax.fori_loop(0, RB * KS, gradient, 0)
     out_s.wait()
     out_m.wait()
 
@@ -522,27 +526,24 @@
     lax.fori_loop(0, NP, drain, 0)
 
 
-def place_kernel(filt, s_in, m_in, g_in, s_out, m_out, g_out, sv, mv, gv, came, went):
-    base = lax.axis_index("col") * CB
+def place_kernel(filt, s_in, m_in, g_in, s_out, m_out, g_out, sv, mv, gv, st, mt, came, went):
     ins = [pltpu.make_async_copy(a, v, came.at[n])
            for n, (a, v) in enumerate(((s_in, sv), (m_in, mv), (g_in, gv)))]
     for c in ins:
         c.start()
     outs = []
-    for n, (v, out) in enumerate(((sv, s_out), (mv, m_out))):
+    for n, (v, to, out) in enumerate(((sv, st, s_out), (mv, mt, m_out))):
         ins[n].wait()
         for i in range(RB):
             for w in range(CB):
-                lanes = pl.ds(pl.multiple_of((filt[i, w] - base) * BS, BS), BS)
-                k = i * CB + w
-                c = pltpu.make_async_copy(
-                    v.at[pl.ds(i * BS, BS), lanes], out.at[k], went.at[n * RB * CB + k])
-                c.start()
-                outs.append(c)
+                lanes = pl.ds(pl.multiple_of(filt[w, i] % CB * BS, BS), BS)
+                to[i * CB + w] = v[pl.ds(i * BS, BS), lanes]
+        outs.append(pltpu.make_async_copy(to, out, went.at[n]))
+        outs[n].start()
     ins[2].wait()
-    c = pltpu.make_async_copy(gv, g_out, went.at[2 * RB * CB])
-    c.start()
-    for c in outs + [c]:
+    outs.append(pltpu.make_async_copy(gv, g_out, went.at[2]))
+    outs[2].start()
+    for c in outs:
         c.wait()
 
 
@@ -584,13 +585,13 @@
             pltpu.VMEM((NP, 2, RB * KS, JP, BS), BF16),
             pltpu.VMEM((NP, RB * KS, JP, BS), BF16),
             pltpu.VMEM((RB * KS, BS, BS), F32),
-            dma(2 + NP), dma(14), dma(14), dma(15), dma(15), dma(HS * NP), dma(HS * NP),
+            dma(2 + NP), dma(14), dma(14), dma(14), dma(14), dma(HS * NP), dma(HS * NP),
             dma(8), dma(8), dma(NP + 2), dma(NP + 2), dma(4 * NP), dma(4 * NP),
             dma(4 * NP), dma(4 * NP), dma(NP), dma(NP),
         ],
         compiler_params=pltpu.CompilerParams(
             collective_id=0, has_side_effects=True, vmem_limit_bytes=67_000_000),
-    )(density.reshape(2, HALF, BS), hamilton.reshape(2, 8, NP, JP, BS), density_cols, hamilton_cols)
+    )(density.reshape(2, HALF, BS), hamilton.reshape(2, 8, NP, JP, BS), density_cols.T, hamilton_cols.T)
     slots = jax.ShapeDtypeStruct((RB * CB, BS, BS), BF16)
     s, m, g = pl.pallas_call(
         place_kernel,
@@ -601,9 +602,11 @@
             pltpu.VMEM((ROWS, COLS), BF16),
             pltpu.VMEM((ROWS, COLS), BF16),
             pltpu.VMEM((RB * KS, BS, BS), BF16),
-            dma(3), dma(2 * RB * CB + 1),
+            pltpu.VMEM((RB * CB, BS, BS), BF16),
+            pltpu.VMEM((RB * CB, BS, BS), BF16),
+            dma(3), dma(3),
         ],
-    )(filter_cols, s, m, g)
+    )(filter_cols.T, s, m, g)
     return (s.reshape(RB, CB, BS, BS), m.reshape(RB, CB, BS, BS), g.reshape(RB, KS, BS, BS))
 
 

time: 116 us -> 111 us (0.957)
  local copies, waits for them, and re-layouts: 2.7 us -> 0 us
    unnamed x9 -> x0, local copies, waits for them, and re-layouts: 2.7 us -> none
where the time goes in v5:
time: 111 us
  Pallas kernels  111 us (100%)
    pallas_call x1, Pallas kernels, local(): pl.pallas_call(kernel, out_shape=(jax.ShapeDtypeStruct((ROWS, COLS), BF16...  107 us
    pallas_call x1, Pallas kernels, local(): pl.pallas_call(place_kernel, out_shape=(slots, slots, jax.ShapeDtypeStruc...  3.71 us

profile of v5, /device:TPU:1, one launch (start us, length us, event | category | flops | bytes accessed | tf_op | source)
XLA Modules:
  0.0 111.2 jit_solution(4696617902100304246)
XLA Ops:
  0.6 106.8 %shard_map.76 = (bf16[1024,512]{1,0:T(8,128)(2,1)}, bf16[1024,512]{1,0:T(8,128)(2,1)}, bf16[16,128,128]{2,1,0:T(8,128)(2,1)}) custom-call(bf16[2,1024,128]{2,1,0:T(8,128)(2,1)} %bitcast.8, bf16[2,8,8,16,128]{4,3,2,1,0:T(8,128)(2,1)} %bitcast.9, s32[2,8]{1,0:T(2,128)} %bitcast.11, s32[2,8]{1,0:T(2,128)} %bitcast.12), custom_call_target="tpu_custom_call" | custom-call | tf_op jit(solution)/shard_map/pallas_call | solution.py:555
  107.5 3.7 %shard_map.77 = (bf16[32,128,128]{2,1,0:T(8,128)(2,1)}, bf16[32,128,128]{2,1,0:T(8,128)(2,1)}, bf16[16,128,128]{2,1,0:T(8,128)(2,1)}) custom-call(s32[4,8]{1,0:T(4,128)} %bitcast.10, bf16[1024,512]{1,0:T(8,128)(2,1)} %get-tuple-element.9.s_in, bf16[1024,512]{1,0:T(8,128)(2,1)} %get-tuple-element.10.m_in, bf16[16,128,128]{2,1,0:T(8,128)(2,1)} %get-tuple-element.11.g_in), custom_call_target="tpu_custom_call" | custom-call | tf_op jit(solution)/shard_map/pallas_call | solution.py:596

commit v6 on v5

--- a/solution.py
+++ b/solution.py
@@ -174,9 +174,9 @@
             n = b0.shape[0] // 16
             for t in range(CB):
                 k = ii * 8 + t
-                i0 = jnp.broadcast_to(ind[k:k + 1], (16, BS)).astype(BF16)
+                i0 = jnp.broadcast_to(ind[k:k + 1], (16, BS)).astype(BF16) > 0.5
                 i1 = jnp.broadcast_to(ind[k + 4:k + 5], (16, BS)).astype(BF16)
-                out = b0.reshape(n, 16, BS) * i0[None] + b1.reshape(n, 16, BS) * i1[None]
+                out = jnp.where(i0[None], b0.reshape(n, 16, BS), b1.reshape(n, 16, BS) * i1[None])
                 store(ii, t, out.reshape(n * 16, BS))
 
     def spread_d(src, k, put):
@@ -301,9 +301,11 @@
     got(dc(1, 1, 1), xr.at[9])
     got(dc(1, -1, 1), xr.at[7])
     got(dc(1, 1, 0), xr.at[8])
-    products(2)
     h_mid(0)
     h_own(3)
+    products(2)
+    h_mid(1)
+    h_own(4)
     products(4)
     got(dc(1, 2, 0), xr.at[12])
     got(dc(1, 2, 1), xr.at[13])
@@ -311,21 +313,24 @@
     got(dr(1, 2, 0), zr.at[12])
     got(dr(1, 2, 1), zr.at[13])
     to_twin(1, 2)
-    h_mid(1)
+    h_mid(2)
     h_far(0)
-    h_own(4)
+    h_own(5)
     product(chunks[6])
+    h_mid(3)
+    h_far(1)
+    h_own(6)
     panel(1, 2, False)
     panel2(1, 2)
+    h_end(0)
+    h_twin(0)
     product(chunks[7])
 
     Sown[...] = accS[...].astype(BF16)
     push(Sown, ts.at[NP], tr.at[NP], twin, Stw)
-    h_mid(2)
-    h_far(1)
-    h_own(5)
-    h_end(0)
-    h_twin(0)
+    h_mid(4)
+    h_far(2)
+    h_own(7)
     out_s = pltpu.make_async_copy(Sown, s_out, loc.at[0])
     out_s.start()
     got(Hti, tr.at[NP + 1])
@@ -344,7 +349,7 @@
         def rows(m, carry):
             def put(ref):
                 def store(ii, t, v):
-                    at = pl.ds(pl.multiple_of(m * 64 + ii * JP, JP), JP)
+                    at = pl.ds(pl.multiple_of(m * (CB * JP) + ii * JP, JP), JP)
                     ref[at, pl.ds(t * BS, BS)] = v
                 return store
             own = Dcol[m, core, pl.ds(SH, IND), :].astype(F32)
@@ -360,18 +365,18 @@
         CT[q % 2] = (
             lax.dot_general(Hr0[...], Sown[...], NT, preferred_element_type=F32)
             + lax.dot_general(Hr1[...], Stw[...], NT, preferred_element_type=F32)
-        )
+        ).astype(BF16)
 
     def extract(q, m, half, emit):
         ind = Drow[2 * m + core, half, pl.ds(HALF, IND), :].astype(F32)
         for ii in range(4):
             lanes = pl.ds((half * 4 + ii) * BS, BS)
-            v = [CT[q % 2, pl.ds(pl.multiple_of(m * 64 + t * JP, JP), JP), lanes] for t in range(CB)]
+            v = [CT[q % 2, pl.ds(pl.multiple_of(m * (CB * JP) + t * JP, JP), JP), lanes] for t in range(CB)]
             for s in range(KS):
                 out = v[0]
                 for t in range(1, CB):
                     k = ii * 8 + s * 4 + t
-                    hit = jnp.broadcast_to(ind[k:k + 1], (JP, BS)) > 0.5
+                    hit = jnp.broadcast_to(ind[k:k + 1], (JP, BS)).astype(BF16) > 0.5
                     out = jnp.where(hit, v[t], out)
                 emit(ii * KS + s, out)
 
@@ -398,7 +403,7 @@
                 for half in (0, 1):
                     def emit(b, v, half=half):
                         if half == side:
-                            v = v + src[q, f, b].astype(F32)
+                            v = v.astype(F32) + src[q, f, b].astype(F32)
                         PB[q, m, half * 8 + b] = v.astype(BF16)
                     extract(q, m, half, emit)
                 remote(PB.at[q, m], dst.at[q, f], bs.at[i], br.at[i], dev).start()
@@ -416,7 +421,7 @@
             got(Bl.at[q, f], br.at[q * 4 + f * 2])
             got(Br.at[q, f], br.at[q * 4 + f * 2 + 1])
             for b in range(RB * KS):
-                v = OWN[q % 3, f, b] + Bl[q, f, b].astype(F32) + Br[q, f, b].astype(F32)
+                v = OWN[q % 3, f, b].astype(F32) + Bl[q, f, b].astype(F32) + Br[q, f, b].astype(F32)
                 if f:
                     PB[q, m, b] = v.astype(BF16)
                 else:
@@ -443,17 +448,13 @@
         return ((ylo + f) % 2) * 4 + (x + d + 4) % 4
 
     def step(q, carry):
-        @pl.when(q + 2 < NP)
-        def _():
-            h_far(q + 2)
+        @pl.when(q + 5 < NP)
+        def _():
+            h_mid(q + 5)
 
         @pl.when(q + 3 < NP)
         def _():
-            h_mid(q + 3)
-
-        @pl.when(q + 6 < NP)
-        def _():
-            h_own(q + 6)
+            h_far(q + 3)
 
         @pl.when(q < NP)
         def _():
@@ -475,14 +476,13 @@
             h_end(q + 1)
             h_twin(q + 1)
 
-        @pl.when(q >= NP - 4)
-        def _():
-            m_chunk(m_order(q - NP + 4))
+        @pl.when(q >= NP - 5)
+        def _():
+            m_chunk(m_order(q - NP + 5))
 
         return carry
 
     lax.fori_loop(0, NP + 3, step, 0)
-    m_chunk(m_order(7))
 
     Mout[...] = accM[...].astype(BF16)
     out_m = pltpu.make_async_copy(Mout, m_out, loc.at[1])
@@ -495,20 +495,6 @@
         return carry
 
     lax.fori_loop(0, RB, direct, 0)
-
-    def y_wait(q, carry):
-        got(Y.at[q], yr.at[q])
-        return carry
-
-    lax.fori_loop(0, NP, y_wait, 0)
-
-    def gradient(b, carry):
-        g_out[b] = (cub[b] - 2.0 * Y[:, b].reshape(BS, BS).astype(F32).T).astype(BF16)
-        return carry
-
-    lax.fori_loop(0, RB * KS, gradient, 0)
-    out_s.wait()
-    out_m.wait()
 
     for c in sends:
         c.wait_send()
@@ -524,6 +510,20 @@
         return carry
 
     lax.fori_loop(0, NP, drain, 0)
+
+    def y_wait(q, carry):
+        got(Y.at[q], yr.at[q])
+        return carry
+
+    lax.fori_loop(0, NP, y_wait, 0)
+
+    def gradient(b, carry):
+        g_out[b] = (cub[b] - 2.0 * Y[:, b].reshape(BS, BS).astype(F32).T).astype(BF16)
+        return carry
+
+    lax.fori_loop(0, RB * KS, gradient, 0)
+    out_s.wait()
+    out_m.wait()
 
 
 def place_kernel(filt, s_in, m_in, g_in, s_out, m_out, g_out, sv, mv, gv, st, mt, came, went):
@@ -576,9 +576,9 @@
             pltpu.VMEM((NR * CB * JP, COLS), BF16),
             pltpu.VMEM((ROWS, COLS), F32),
             pltpu.VMEM((ROWS, COLS), F32),
-            pltpu.VMEM((2, NR * CB * JP, ROWS), F32),
+            pltpu.VMEM((2, NR * CB * JP, ROWS), BF16),
             pltpu.VMEM((NP, NR, RB * KS, JP, BS), BF16),
-            pltpu.VMEM((3, 2, RB * KS, JP, BS), F32),
+            pltpu.VMEM((3, 2, RB * KS, JP, BS), BF16),
             pltpu.VMEM((NP, 2, RB, JP, BS), BF16),
             pltpu.VMEM((NP, 2, RB, JP, BS), BF16),
             pltpu.VMEM((NP, 2, RB * KS, JP, BS), BF16),

time: 111 us -> 109 us (0.982)
  Pallas kernels: 111 us -> 108 us
    pallas_call x1, Pallas kernels: 107 us -> 105 us  [local(): pl.pallas_call(kernel, out_shape=(jax.ShapeDtypeStruct((ROWS, COLS), BF16...]
where the time goes in v6:
time: 109 us
  Pallas kernels  108 us (99%)
    pallas_call x1, Pallas kernels, local(): pl.pallas_call(kernel, out_shape=(jax.ShapeDtypeStruct((ROWS, COLS), BF16...  105 us
    pallas_call x1, Pallas kernels, local(): pl.pallas_call(place_kernel, out_shape=(slots, slots, jax.ShapeDtypeStruc...  3.71 us

profile of v6, /device:TPU:1, one launch (start us, length us, event | category | flops | bytes accessed | tf_op | source)
XLA Modules:
  0.0 109.1 jit_solution(691025447521799104)
XLA Ops:
  0.6 104.8 %shard_map.76 = (bf16[1024,512]{1,0:T(8,128)(2,1)}, bf16[1024,512]{1,0:T(8,128)(2,1)}, bf16[16,128,128]{2,1,0:T(8,128)(2,1)}) custom-call(bf16[2,1024,128]{2,1,0:T(8,128)(2,1)} %bitcast.8, bf16[2,8,8,16,128]{4,3,2,1,0:T(8,128)(2,1)} %bitcast.9, s32[2,8]{1,0:T(2,128)} %bitcast.11, s32[2,8]{1,0:T(2,128)} %bitcast.12), custom_call_target="tpu_custom_call" | custom-call | tf_op jit(solution)/shard_map/pallas_call | solution.py:555
  105.4 3.7 %shard_map.77 = (bf16[32,128,128]{2,1,0:T(8,128)(2,1)}, bf16[32,128,128]{2,1,0:T(8,128)(2,1)}, bf16[16,128,128]{2,1,0:T(8,128)(2,1)}) custom-call(s32[4,8]{1,0:T(4,128)} %bitcast.10, bf16[1024,512]{1,0:T(8,128)(2,1)} %get-tuple-element.9.s_in, bf16[1024,512]{1,0:T(8,128)(2,1)} %get-tuple-element.10.m_in, bf16[16,128,128]{2,1,0:T(8,128)(2,1)} %get-tuple-element.11.g_in), custom_call_target="tpu_custom_call" | custom-call | tf_op jit(solution)/shard_map/pallas_call | solution.py:596
